TPU v7x, 256 devices: a whole 4x4x8 slice. The times are simulated.
256 devices in a mesh: struct: 16 (over z, x_hi), atom: 16 (over x_lo, y, core).
Axes of the slice: x: 4 (x_hi: 2, x_lo: 2; x = x_hi * 2 + x_lo), y: 4, z: 8, core: 2. Of those that a mesh axis runs over, the one named last changes fastest.
Arguments:
- atoms_in: bfloat16 [64, 6144, 128], P('struct', 'atom'), parts along dimension 0, may hold values from -6 to 6
- cond: bfloat16 [98304, 128], P(('struct', 'atom')), parts along dimension 0, may hold values from -6 to 6
- pair: bfloat16 [3072, 32, 16, 128], P(('struct', 'atom')), parts along dimension 0, may hold values from -6 to 6
- atom_mask: int32 [98304], P(('struct', 'atom')), parts along dimension 0, may hold values 0 or 1
- atom_count: int32 [16], P('struct'), parts along dimension 0, may hold values from 5952 to 6144
- atom_to_token: int32 [98304], P(('struct', 'atom')), parts along dimension 0, may hold values from 0 to 767, as said below
- ada_weight: bfloat16 [2, 128, 256], replicated, may hold values from -0.5 to 0.5
- ada_bias: float32 [2, 128], replicated, may hold values from -1.5 to 1.5
- zero_weight: bfloat16 [2, 128, 128], replicated, may hold values from -0.5 to 0.5
- zero_bias: float32 [2, 128], replicated, may hold values from -2 to 2
- qkvg_weight: bfloat16 [128, 512], replicated, may hold values from -0.5 to 0.5
- query_bias: float32 [128], replicated, may hold values from -4 to 4
- pair_weight: float32 [4, 16], replicated, may hold values from -60 to 60
- out_weight: bfloat16 [128, 128], replicated, may hold values from -0.5 to 0.5
- swiglu_weight: bfloat16 [128, 512], replicated, may hold values from -0.5 to 0.5
- down_weight: bfloat16 [256, 128], replicated, may hold values from -0.375 to 0.375
- token_weight: bfloat16 [128, 768], replicated, may hold values from -0.5 to 0.5
Outputs:
- atoms_out: bfloat16 [64, 6144, 128], P('struct', 'atom'), parts along dimension 0
- tokens_out: bfloat16 [64, 768, 768], P('struct', 'atom'), parts along dimension 0
There are 16 independent parts, one for each index of `struct`. A program takes and returns all parts, laid end to end along the dimension named above; an argument that names none is the same for every part. Nothing has to cross between parts.
Inputs may be any that keep to these rules, and one draw needn't show every extreme that they name: `atom_to_token`: never falls, rises by at most 1 from atom to atom, starts at 0 and ends at 767; an atom a of token t satisfies 8 * t - 8 < a < 8 * t + 2 * 8 - 1.
All inputs are finite; a program needn't handle non-finite values. No bound on the sum of `atom_mask` on one device may be relied on, other than what follows from the above.
Results may differ from a plain program's by a relative error of at most 0.01.
Values may be sent and summed in bfloat16 or wider, within the bound.
No kernel may reach another device: no remote copies, remote signals or barrier semaphores. Data moves between devices by JAX's collectives and lax.ppermute only.
A program may use at most 64 MiB of HBM per device.

v0:
```python
import jax
import jax.numpy as jnp
from jax import lax
from jax.sharding import PartitionSpec as P

ATOMS_PER_TOKEN = 8


EPS = 1e-05


def extended_2(shard, sides, width):
    for axis, dim in sides:
        count, length = (lax.axis_size(axis), shard.shape[dim])
        up = [(i, (i + 1) % count) for i in range(count - 1)]
        down = [(j, i) for i, j in up]
        last = lax.slice_in_dim(shard, length - width, length, axis=dim)
        initial = lax.slice_in_dim(shard, 0, width, axis=dim)
        before = lax.ppermute(last, axis, up)
        after = lax.ppermute(initial, axis, down)
        shard = jnp.concatenate([before, shard, after], axis=dim)
    return shard


def layer_norm(values, along=-1):
    center = jnp.mean(values, along, keepdims=True)
    spread = jnp.mean(jnp.square(values - center), along, keepdims=True)
    return (values - center) * lax.rsqrt(spread + EPS)


def window_view(extended, windows_here, query_len, reach):
    blocks = extended.reshape(
        (extended.shape[0], windows_here + reach - 1, query_len) + extended.shape[2:]
    )
    return jnp.concatenate(
        [blocks[:, offset : offset + windows_here] for offset in range(reach)], axis=2
    )


def on_device(
    atoms_in,
    cond,
    pair,
    atom_mask,
    atom_count,
    atom_to_token,
    ada_weight,
    ada_bias,
    zero_weight,
    zero_bias,
    qkvg_weight,
    query_bias,
    pair_weight,
    out_weight,
    swiglu_weight,
    down_weight,
    token_weight,
):
    samples, atom_dev, model_width = atoms_in.shape
    head_count = pair_weight.shape[0]
    head_dim = model_width // head_count
    query_len = pair.shape[1]
    key_len = pair.shape[3]
    reach = key_len // query_len
    margin = (key_len - query_len) // 2
    windows_here = atom_dev // query_len
    tok_dev = atom_dev // ATOMS_PER_TOKEN
    device_pos = lax.axis_index("atom")
    start_atom = device_pos * atom_dev
    atoms_total = lax.axis_size("atom") * atom_dev
    integers = jnp.stack([atom_mask, atom_to_token])
    integers_ext = extended_2(integers, (("atom", 1),), margin)
    ext_positions = start_atom - margin + jnp.arange(atom_dev + 2 * margin, dtype=jnp.int32)
    usable_ext = (
        (integers_ext[0] == 1)
        & (ext_positions >= 0)
        & (ext_positions < atoms_total)
        & (ext_positions < atom_count[0])
    )
    usable_local = usable_ext[margin : margin + atom_dev]
    cond_norm = layer_norm(cond.astype(jnp.float32)).astype(jnp.bfloat16)
    adapt = [
        jnp.dot(cond_norm, ada_weight[which], preferred_element_type=jnp.float32)
        for which in range(2)
    ]
    gating = [
        jax.nn.sigmoid(
            jnp.dot(cond_norm, zero_weight[which], preferred_element_type=jnp.float32)
            + zero_bias[which]
        )
        for which in range(2)
    ]

    def adaptive(stream, which):
        return (
            layer_norm(stream) * jax.nn.sigmoid(adapt[which][:, :model_width] + ada_bias[which])
            + adapt[which][:, model_width:]
        )

    attn_in = adaptive(atoms_in.astype(jnp.float32), 0).astype(jnp.bfloat16)
    projected = jnp.dot(attn_in, qkvg_weight, preferred_element_type=jnp.float32)
    factor = head_dim ** (-0.5)
    queries = ((projected[..., :model_width] + query_bias) * factor).astype(jnp.bfloat16)
    gate_attn = jax.nn.sigmoid(projected[..., 3 * model_width :])
    keyval_local = projected[..., model_width : 3 * model_width].astype(jnp.bfloat16)
    keyval = extended_2(keyval_local, (("atom", 1),), margin)
    windowed = window_view(keyval, windows_here, query_len, reach)
    key_live = window_view(usable_ext[None], windows_here, query_len, reach)[0]
    pair_norm = layer_norm(pair.astype(jnp.float32), 2)
    pair_bias = jnp.einsum("wicj,hc->whij", pair_norm, pair_weight, precision=lax.Precision.HIGHEST)
    query_win = queries.reshape(samples, windows_here, query_len, head_count, head_dim)
    keys_win = windowed[..., :model_width].reshape(
        samples, windows_here, key_len, head_count, head_dim
    )
    values_win = windowed[..., model_width:].reshape(
        samples, windows_here, key_len, head_count, head_dim
    )
    scores = (
        jnp.einsum("bwihd,bwjhd->bwhij", query_win, keys_win, preferred_element_type=jnp.float32)
        + pair_bias[None]
    )
    scores = jnp.where(key_live[None, :, None, None, :], scores, -1000000000.0)
    attention = jax.nn.softmax(scores, axis=-1).astype(jnp.bfloat16)
    weighted = jnp.einsum(
        "bwhij,bwjhd->bwihd", attention, values_win, preferred_element_type=jnp.float32
    )
    blended = (weighted.reshape(samples, atom_dev, model_width) * gate_attn).astype(jnp.bfloat16)
    after_attn = (
        atoms_in.astype(jnp.float32)
        + gating[0] * jnp.dot(blended, out_weight, preferred_element_type=jnp.float32)
    ).astype(jnp.bfloat16)
    trans_in = adaptive(after_attn.astype(jnp.float32), 1).astype(jnp.bfloat16)
    mixed = jnp.dot(trans_in, swiglu_weight, preferred_element_type=jnp.float32)
    hidden_units = mixed.shape[-1] // 2
    hidden = (jax.nn.silu(mixed[..., :hidden_units]) * mixed[..., hidden_units:]).astype(
        jnp.bfloat16
    )
    atoms_out = (
        after_attn.astype(jnp.float32)
        + gating[1] * jnp.dot(hidden, down_weight, preferred_element_type=jnp.float32)
    ).astype(jnp.bfloat16)
    features = jax.nn.relu(
        jnp.dot(atoms_out, token_weight, preferred_element_type=jnp.float32)
    ).astype(jnp.bfloat16)
    token_base = device_pos * tok_dev - 1
    slots = jnp.arange(tok_dev + 2, dtype=jnp.int32)
    relative_local = atom_to_token - token_base
    onehot_local = ((relative_local[:, None] == slots[None, :]) & usable_local[:, None]).astype(
        jnp.bfloat16
    )
    totals = jnp.einsum("at,bac->btc", onehot_local, features, preferred_element_type=jnp.float32)
    relative_ext = integers_ext[1] - token_base
    counts = jnp.sum(
        ((relative_ext[:, None] == slots[None, :]) & usable_ext[:, None]).astype(jnp.float32),
        axis=0,
    )
    lower_row = totals[:, 0]
    upper_row = totals[:, tok_dev + 1]
    edges_sums = extended_2(jnp.stack([lower_row, upper_row], axis=1), (("atom", 1),), 1)
    from_left = edges_sums[:, 0]
    from_right = edges_sums[:, 3]
    local_rows = totals[:, 1 : tok_dev + 1]
    first_row = local_rows[:, :1] + from_left[:, None]
    last_row = local_rows[:, tok_dev - 1 :] + from_right[:, None]
    local_rows = jnp.concatenate([first_row, local_rows[:, 1 : tok_dev - 1], last_row], axis=1)
    tokens_out = (local_rows / jnp.maximum(counts[1 : tok_dev + 1], 1.0)[None, :, None]).astype(
        jnp.bfloat16
    )
    return (atoms_out, tokens_out)


def solution(mesh):
    in_specs = (
        P("struct", "atom", None),
        P(("struct", "atom"), None),
        P(("struct", "atom"), None, None, None),
        P(("struct", "atom")),
        P("struct"),
        P(("struct", "atom")),
        P(),
        P(),
        P(),
        P(),
        P(),
        P(),
        P(),
        P(),
        P(),
        P(),
        P(),
    )
    out_specs = (P("struct", "atom", None), P("struct", "atom", None))
    return jax.shard_map(
        on_device, mesh=mesh, in_specs=in_specs, out_specs=out_specs, check_vma=False
    )
```

profile of v0, /device:TPU:189, one launch (start us, length us, event | category | flops | bytes accessed | tf_op | source)
XLA Modules:
  0.0 72.7 jit_solution(4648647374006792727)
XLA Ops:
  0.7 1.1 %convert_reduce_fusion.2 = f32[384]{0:T(512)S(1)} fusion(bf16[384,128]{1,0:T(8,128)(2,1)} %param.18), kind=kLoop, calls=%fused_computation.80 | loop fusion | flops 97920 | bytes 99840 | tf_op jit(solution)/shard_map/reduce_sum | solution.py:26
  1.7 1.1 %fusion.67 = f32[384]{0:T(512)S(1)} fusion(bf16[384,128]{1,0:T(8,128)(2,1)} %param.18, f32[384]{0:T(512)S(1)} %broadcast_multiply_fusion.3), kind=kLoop, calls=%fused_computation.83 | loop fusion | flops 196224 | bytes 101376 | tf_op jit(solution)/shard_map/reduce_sum | solution.py:27
  2.9 1.2 %fusion.86 = f32[384,256]{1,0:T(8,128)S(1)} fusion(bf16[2,128,256]{2,1,0:T(8,128)(2,1)} %param.23, bf16[384,128]{1,0:T(8,128)(2,1)} %param.18, f32[384]{0:T(512)S(1)} %add_rsqrt_fusion.3, f32[384]{0:T(512)S(1)} %broadcast_multiply_fusion.3), kind=kOutput, calls=%fused_computation.107 | convolution fusion | flops 25362432 | bytes 560128 | tf_op jit(solution)/shard_map/dot_general | solution.py:83
  4.1 1.2 %fusion.88 = f32[384,256]{1,0:T(8,128)S(1)} fusion(bf16[2,128,256]{2,1,0:T(8,128)(2,1)} %param.23, bf16[384,128]{1,0:T(8,128)(2,1)} %param.18, f32[384]{0:T(512)S(1)} %add_rsqrt_fusion.3, f32[384]{0:T(512)S(1)} %broadcast_multiply_fusion.3), kind=kOutput, calls=%fused_computation.109 | convolution fusion | flops 25362432 | bytes 560128 | tf_op jit(solution)/shard_map/dot_general | solution.py:83
  5.2 1.2 %copy.36 = bf16[4,384,128]{1,2,0:T(8,128)(2,1)S(1)} copy(bf16[4,384,128]{2,1,0:T(8,128)(2,1)} %param.17) | data formatting | bytes 786432 | tf_op args[0]
  6.5 0.8 %slice_bitcast_fusion = (f32[128]{0:T(128)S(1)}, f32[128]{0:T(128)S(1)}) fusion(f32[2,128]{1,0:T(2,128)} %param.24), kind=kLoop, calls=%fused_computation.151 | loop fusion | bytes 2048 | tf_op jit(solution)/shard_map/add | solution.py:96
  7.5 0.1 copy.38
  7.9 0.6 fusion.124
  8.6 0.7 fusion.121
  9.2 2.8 %collective-permute-start.1 = (bf16[4,48,256]{2,1,0:T(8,128)(2,1)}, bf16[4,48,256]{2,1,0:T(8,128)(2,1)}, u32[]{:S(2)}, u32[]{:S(2)}) collective-permute-start(bf16[4,48,256]{2,1,0:T(8,128)(2,1)} %get-tuple-element.9), channel_id=1, source_target_pairs={{1,0},{2,1},{3,2},{4,3},{5,4},{6,5},{7,6},{8,7},{9,8},{10,9},{11,1... | collective-permute-start | bytes 294920 | tf_op jit(solution)/shard_map/ppermute | solution.py:20
  12.1 5.1 %collective-permute-start = (bf16[4,48,256]{2,1,0:T(8,128)(2,1)}, bf16[4,48,256]{2,1,0:T(8,128)(2,1)}, u32[]{:S(2)}, u32[]{:S(2)}) collective-permute-start(bf16[4,48,256]{2,1,0:T(8,128)(2,1)} %get-tuple-element.8), channel_id=1, source_target_pairs={{0,1},{1,2},{2,3},{3,4},{4,5},{5,6},{6,7},{7,8},{8,9},{9,10},{10,1... | collective-permute-start | bytes 294920 | tf_op jit(solution)/shard_map/ppermute | solution.py:19
  17.2 0.7 pad_add_fusion.2
  17.9 1.9 %collective-permute-start.3 = (s32[2,48]{1,0:T(2,128)}, s32[2,48]{1,0:T(2,128)S(1)}, u32[]{:S(2)}, u32[]{:S(2)}) collective-permute-start(s32[2,48]{1,0:T(2,128)} %get-tuple-element.21), channel_id=1, source_target_pairs={{1,0},{2,1},{3,2},{4,3},{5,4},{6,5},{7,6},{8,7},{9,8},{10,9},{11,1... | collective-permute-start | bytes 1160 | tf_op jit(solution)/shard_map/ppermute | solution.py:20
  19.8 5.8 %collective-permute-start.2 = (s32[2,48]{1,0:T(2,128)}, s32[2,48]{1,0:T(2,128)}, u32[]{:S(2)}, u32[]{:S(2)}) collective-permute-start(s32[2,48]{1,0:T(2,128)} %get-tuple-element.20), channel_id=1, source_target_pairs={{0,1},{1,2},{2,3},{3,4},{4,5},{5,6},{6,7},{7,8},{8,9},{9,10},{10,1... | collective-permute-start | bytes 1160 | tf_op jit(solution)/shard_map/ppermute | solution.py:19
  25.8 1.8 %reshape.153 = bf16[4,12,32,4,32]{4,3,2,1,0:T(4,128)(2,1)} reshape(bf16[4,384,128]{2,1,0:T(8,128)(2,1)S(1)} %fusion.48) | data formatting | bytes 786432 | tf_op jit(solution)/shard_map/reshape | solution.py:111
  27.6 0.7 %convert_reduce_fusion = f32[12,32,128]{2,1,0:T(8,128)S(1)} fusion(bf16[12,32,16,128]{3,2,1,0:T(8,128)(2,1)S(1)} %copy-done.1), kind=kLoop, calls=%fused_computation.3 | loop fusion | flops 1523712 | bytes 1769472 | tf_op jit(solution)/shard_map/reduce_sum | solution.py:26
  28.4 1.0 %fusion.3 = f32[12,32,128]{2,1,0:T(8,128)S(1)} fusion(bf16[12,32,16,128]{3,2,1,0:T(8,128)(2,1)S(1)} %copy-done.1, f32[12,32,128]{2,1,0:T(8,128)S(1)} %broadcast_multiply_fusion), kind=kLoop, calls=%fused_computation.6 | loop fusion | flops 3096576 | bytes 1966080 | tf_op jit(solution)/shard_map/reduce_sum | solution.py:27
  29.4 2.0 %fusion.20 = f32[12,4,32,128]{3,1,2,0:T(4,128)S(1)} fusion(bf16[12,32,16,128]{3,2,1,0:T(8,128)(2,1)S(1)} %copy-done.1, f32[12,32,128]{2,1,0:T(8,128)S(1)} %add_rsqrt_fusion, f32[12,32,128]{2,1,0:T(8,128)S(1)} %broadcast_multiply_fusion, f32[4,16]{1,0:T(4,128)S(1)} %copy-done.12), kind=kOutput, calls=%fused_computation.27 | convolution fusion | flops 40108032 | bytes 2752768 | tf_op jit(solution)/shard_map/wicj,hc->whij/dot_general | solution.py:110
  31.4 1.0 %copy.44 = f32[12,4,32,128]{3,2,1,0:T(8,128)} copy(f32[12,4,32,128]{3,1,2,0:T(4,128)S(1)} %fusion.20) | data formatting | bytes 1572864 | tf_op jit(solution)/shard_map/wicj,hc->whij/transpose | solution.py:110
  33.1 0.3 fusion.32
  33.4 0.8 %copy.37 = f32[384,128]{0,1:T(8,128)} copy(f32[384,128]{1,0:T(8,128)S(1)} %fusion.32) | data formatting | bytes 393216 | tf_op jit(solution)/shard_map/div | solution.py:87
  34.2 0.3 fusion.36
  34.7 0.8 %copy.48 = f32[384,128]{0,1:T(8,128)} copy(f32[384,128]{1,0:T(8,128)S(1)} %get-tuple-element.16) | data formatting | bytes 393216 | tf_op jit(solution)/shard_map/div | solution.py:87
  35.5 0.8 %copy.47 = f32[384,128]{0,1:T(8,128)} copy(f32[384,128]{1,0:T(8,128)S(1)} %fusion.36) | data formatting | bytes 393216 | tf_op jit(solution)/shard_map/div | solution.py:87
  36.3 0.7 pad_add_fusion
  37.2 0.7 slice.159
  37.9 1.0 %pad_maximum_fusion.1 = bf16[4,480,256]{2,1,0:T(8,128)(2,1)S(1)} fusion(bf16[4,48,256]{2,1,0:T(8,128)(2,1)} %collective-permute-done.1, bf16[4,384,256]{2,1,0:T(8,128)(2,1)S(1)} %slice.170, bf16[4,48,256]{2,1,0:T(8,128)(2,1)} %collective-permute-done), kind=kLoop, calls=%fused_computation.48 | loop fusion | flops 2949120 | bytes 1966080 | tf_op jit(solution)/shard_map/concatenate | solution.py:21
  39.0 0.4 fusion.122
  39.4 0.5 pad_maximum_fusion
  39.9 0.9 %fusion.120 = (bf16[4,12,128,128]{3,2,1,0:T(8,128)(2,1)S(1)}, bf16[4,12,128,128]{3,2,1,0:T(8,128)(2,1)S(1)}) fusion(bf16[4,12,128,256]{3,2,1,0:T(8,128)(2,1)S(1)} %pad_maximum_fusion), kind=kLoop, calls=%fused_computation.159 | loop fusion | bytes 6291456 | tf_op jit(solution)/shard_map/slice | solution.py:112
  40.8 1.6 %copy.41 = bf16[4,12,128,128]{2,3,1,0:T(8,128)(2,1)} copy(bf16[4,12,128,128]{3,2,1,0:T(8,128)(2,1)S(1)} %get-tuple-element.7) | data formatting | bytes 3145728 | tf_op jit(solution)/shard_map/slice | solution.py:115
  42.4 0.9 %copy.42 = bf16[4,12,128,128]{2,3,1,0:T(8,128)(2,1)S(1)} copy(bf16[4,12,128,128]{3,2,1,0:T(8,128)(2,1)S(1)} %get-tuple-element.6) | data formatting | bytes 3145728 | tf_op jit(solution)/shard_map/slice | solution.py:112
  43.3 2.0 %fusion.12 = f32[4,12,4,32,128]{4,3,2,1,0:T(8,128)S(1)} fusion(bf16[4,12,128,4,32]{2,4,3,1,0:T(8,128)(2,1)S(1)} %bitcast.67, bf16[4,12,32,4,32]{4,3,2,1,0:T(4,128)(2,1)} %reshape.153), kind=kOutput, calls=%fused_computation.19 | convolution fusion | flops 50331648 | bytes 5111808 | tf_op jit(solution)/shard_map/bwihd,bwjhd->bwhij/dot_general | solution.py:119
  45.4 3.0 %fusion.125 = (f32[4,12,4,32]{3,2,1,0:T(4,128)S(1)}, f32[4,12,4,32,128]{4,3,2,1,0:T(8,128)S(1)}) fusion(f32[4,12,4,32,128]{4,3,2,1,0:T(8,128)S(1)} %fusion.12, f32[12,4,32,128]{3,2,1,0:T(8,128)S(1)} %copy-done.4, pred[12,128]{1,0:T(8,128)(4,1)S(1)} %add_bitcast_fusion), kind=kOutput, calls=%fused_computation.164 | output fusion | flops 4718719 | bytes 7104000 | tf_op jit(solution)/shard_map/sub | solution.py:123
  48.5 2.4 %convolution_bitcast_fusion = f32[4,12,32,4,32]{2,4,3,1,0:T(8,128)} fusion(bf16[4,12,128,4,32]{2,4,3,1,0:T(8,128)(2,1)S(1)} %bitcast.68, f32[4,12,4,32,128]{4,3,2,1,0:T(8,128)S(1)} %get-tuple-element.33, f32[4,12,4,32]{3,2,1,0:T(4,128)S(1)} %get-tuple-element.32), kind=kOutput, calls=%fused_computation.16 | convolution fusion | flops 51904512 | bytes 5529600 | tf_op jit(solution)/shard_map/bwhij,bwjhd->bwihd/dot_general | solution.py:124
  50.9 3.3 %copy.45 = f32[4,12,32,4,32]{4,3,2,1,0:T(4,128)S(1)} copy(f32[4,12,32,4,32]{2,4,3,1,0:T(8,128)} %convolution_bitcast_fusion) | data formatting | bytes 1572864 | tf_op jit(solution)/shard_map/bwhij,bwjhd->bwihd/transpose | solution.py:124
  54.2 2.2 %reshape.155 = f32[4,384,128]{2,1,0:T(8,128)} reshape(f32[4,12,32,4,32]{4,3,2,1,0:T(4,128)S(1)} %copy.45) | data formatting | bytes 1572864 | tf_op jit(solution)/shard_map/reshape | solution.py:127
  56.3 2.0 %fusion.126 = (f32[4,384]{1,0:T(4,128)S(1)}, f32[4,384,128]{1,2,0:T(8,128)S(1)}) fusion(bf16[128,128]{1,0:T(8,128)(2,1)} %param.30, f32[4,384,128]{2,1,0:T(8,128)} %reshape.155, f32[4,384,512]{2,1,0:T(8,128)} %copy-done.3, f32[384,128]{0,1:T(8,128)} %copy.37, bf16[4,384,128]{1,2,0:T(8,128)(2,1)} %copy-done.2), kind=kOutput, calls=%fused_computation.165 | convolution fusion | flops 52492800 | bytes 2988032 | tf_op jit(solution)/shard_map/dot_general | solution.py:130
  58.5 0.6 fusion.53
  59.2 0.1 copy-done.8
  59.3 0.7 fusion.28
  60.0 1.3 %fusion.25 = f32[4,50,768]{2,1,0:T(8,128)S(1)} fusion(bf16[4,384,128]{1,2,0:T(8,128)(2,1)S(1)} %fusion.28, bf16[128,768]{1,0:T(8,128)(2,1)S(1)} %copy-done, s32[384]{0:T(512)S(1)} %broadcast_subtract_fusion, pred[384]{0:T(512)(128)(4,1)S(1)} %copy-done.18), kind=kOutput, calls=%fused_computation.32 | convolution fusion | flops 422352384 | bytes 1206144 | tf_op jit(solution)/shard_map/at,bac->btc/dot_general | solution.py:151
  61.4 1.9 %collective-permute-start.4 = (f32[4,1,768]{2,1,0:T(1,128)S(1)}, f32[4,1,768]{2,1,0:T(1,128)S(1)}, u32[]{:S(2)}, u32[]{:S(2)}) collective-permute-start(f32[4,1,768]{2,1,0:T(1,128)S(1)} %slice.190), channel_id=1, source_target_pairs={{0,1},{1,2},{2,3},{3,4},{4,5},{5,6},{6,7},{7,8},{8,9},{9,10},{10,1... | collective-permute-start | bytes 36872 | tf_op jit(solution)/shard_map/ppermute | solution.py:19
  63.4 1.0 %collective-permute-done.4 = f32[4,1,768]{2,1,0:T(1,128)S(1)} collective-permute-done((f32[4,1,768]{2,1,0:T(1,128)S(1)}, f32[4,1,768]{2,1,0:T(1,128)S(1)}, u32[]{:S(2)}, u32[]{:S(2)}) %collective-permute-start.4) | collective-permute-done | bytes 12320 | tf_op jit(solution)/shard_map/ppermute | solution.py:19
  64.5 2.1 %collective-permute-start.5 = (f32[4,1,768]{2,1,0:T(1,128)S(1)}, f32[4,1,768]{2,1,0:T(1,128)S(1)}, u32[]{:S(2)}, u32[]{:S(2)}) collective-permute-start(f32[4,1,768]{2,1,0:T(1,128)S(1)} %get-tuple-element.15), channel_id=1, source_target_pairs={{1,0},{2,1},{3,2},{4,3},{5,4},{6,5},{7,6},{8,7},{9,8},{10,9},{11,1... | collective-permute-start | bytes 36872 | tf_op jit(solution)/shard_map/ppermute | solution.py:20
  66.6 0.9 %copy.52 = bf16[4,384,128]{2,1,0:T(8,128)(2,1)} copy(bf16[4,384,128]{1,2,0:T(8,128)(2,1)S(1)} %fusion.28) | data formatting | bytes 786432
  67.6 4.2 %collective-permute-done.5 = f32[4,1,768]{2,1,0:T(1,128)S(1)} collective-permute-done((f32[4,1,768]{2,1,0:T(1,128)S(1)}, f32[4,1,768]{2,1,0:T(1,128)S(1)}, u32[]{:S(2)}, u32[]{:S(2)}) %collective-permute-start.5) | collective-permute-done | bytes 12320 | tf_op jit(solution)/shard_map/ppermute | solution.py:20
  71.8 0.8 %fusion.51 = bf16[4,48,768]{2,1,0:T(8,128)(2,1)} fusion(f32[4,1,768]{2,1,0:T(1,128)S(1)} %slice_add_fusion.3, f32[4,46,768]{2,1,0:T(8,128)S(1)} %slice.191, f32[4,1,768]{2,1,0:T(1,128)S(1)} %get-tuple-element.14, f32[48]{0:T(128)S(1)} %slice_maximum_fusion), kind=kLoop, calls=%fused_computation.67 | loop fusion | flops 589824 | bytes 884928 | tf_op jit(solution)/shard_map/convert_element_type | solution.py:166
  (74 shorter events, 1.6 us)
Async XLA Ops:
  0.6 59.3 %copy-start = (bf16[128,768]{1,0:T(8,128)(2,1)S(1)}, bf16[128,768]{1,0:T(8,128)(2,1)}, u32[]{:S(2)}) copy-start(bf16[128,768]{1,0:T(8,128)(2,1)} %param.33) | copy-start | bytes 589828
  0.6 7.2 %copy-start.9 = (bf16[128,512]{1,0:T(8,128)(2,1)S(1)}, bf16[128,512]{1,0:T(8,128)(2,1)}, u32[]{:S(2)}) copy-start(bf16[128,512]{1,0:T(8,128)(2,1)} %param.27) | copy-start | bytes 393220
  6.5 1.4 %copy-start.2 = (bf16[4,384,128]{1,2,0:T(8,128)(2,1)}, bf16[4,384,128]{1,2,0:T(8,128)(2,1)S(1)}, u32[]{:S(2)}) copy-start(bf16[4,384,128]{1,2,0:T(8,128)(2,1)S(1)} %copy.36) | copy-start | bytes 1179652
  7.7 9.5 %copy-start.11 = (s32[384]{0:T(512)S(1)}, s32[384]{0:T(512)}, u32[]{:S(2)}) copy-start(s32[384]{0:T(512)} %param.22) | copy-start | bytes 4612
  7.7 9.5 %copy-start.13 = (s32[384]{0:T(512)S(1)}, s32[384]{0:T(512)}, u32[]{:S(2)}) copy-start(s32[384]{0:T(512)} %param.20) | copy-start | bytes 4612
  7.9 17.7 %copy-start.15 = (f32[128]{0:T(128)S(1)}, f32[128]{0:T(128)}, u32[]{:S(2)}) copy-start(f32[128]{0:T(128)} %param.28) | copy-start | bytes 1540
  8.5 17.1 %copy-start.3 = (f32[4,384,512]{2,1,0:T(8,128)}, f32[4,384,512]{2,1,0:T(8,128)S(1)}, u32[]{:S(2)}) copy-start(f32[4,384,512]{2,1,0:T(8,128)S(1)} %get-tuple-element.31) | copy-start | bytes 9437188
  8.5 19.0 %copy-start.1 = (bf16[12,32,16,128]{3,2,1,0:T(8,128)(2,1)S(1)}, bf16[12,32,16,128]{3,2,1,0:T(8,128)(2,1)}, u32[]{:S(2)}) copy-start(bf16[12,32,16,128]{3,2,1,0:T(8,128)(2,1)} %param.19) | copy-start | bytes 4718596
  9.2 28.7 %collective-permute-start.1 = (bf16[4,48,256]{2,1,0:T(8,128)(2,1)}, bf16[4,48,256]{2,1,0:T(8,128)(2,1)}, u32[]{:S(2)}, u32[]{:S(2)}) collective-permute-start(bf16[4,48,256]{2,1,0:T(8,128)(2,1)} %get-tuple-element.9), channel_id=1, source_target_pairs={{1,0},{2,1},{3,2},{4,3},{5,4},{6,5},{7,6},{8,7},{9,8},{10,9},{11,1... | collective-permute-start | bytes 294920 | tf_op jit(solution)/shard_map/ppermute | solution.py:20
  12.1 25.9 %collective-permute-start = (bf16[4,48,256]{2,1,0:T(8,128)(2,1)}, bf16[4,48,256]{2,1,0:T(8,128)(2,1)}, u32[]{:S(2)}, u32[]{:S(2)}) collective-permute-start(bf16[4,48,256]{2,1,0:T(8,128)(2,1)} %get-tuple-element.8), channel_id=1, source_target_pairs={{0,1},{1,2},{2,3},{3,4},{4,5},{5,6},{6,7},{7,8},{8,9},{9,10},{10,1... | collective-permute-start | bytes 294920 | tf_op jit(solution)/shard_map/ppermute | solution.py:19
  17.9 18.4 %collective-permute-start.3 = (s32[2,48]{1,0:T(2,128)}, s32[2,48]{1,0:T(2,128)S(1)}, u32[]{:S(2)}, u32[]{:S(2)}) collective-permute-start(s32[2,48]{1,0:T(2,128)} %get-tuple-element.21), channel_id=1, source_target_pairs={{1,0},{2,1},{3,2},{4,3},{5,4},{6,5},{7,6},{8,7},{9,8},{10,9},{11,1... | collective-permute-start | bytes 1160 | tf_op jit(solution)/shard_map/ppermute | solution.py:20
  19.8 16.5 %collective-permute-start.2 = (s32[2,48]{1,0:T(2,128)}, s32[2,48]{1,0:T(2,128)}, u32[]{:S(2)}, u32[]{:S(2)}) collective-permute-start(s32[2,48]{1,0:T(2,128)} %get-tuple-element.20), channel_id=1, source_target_pairs={{0,1},{1,2},{2,3},{3,4},{4,5},{5,6},{6,7},{7,8},{8,9},{9,10},{10,1... | collective-permute-start | bytes 1160 | tf_op jit(solution)/shard_map/ppermute | solution.py:19
  25.8 3.6 %copy-start.12 = (f32[4,16]{1,0:T(4,128)S(1)}, f32[4,16]{1,0:T(4,128)}, u32[]{:S(2)}) copy-start(f32[4,16]{1,0:T(4,128)} %param.29) | copy-start | bytes 772
  28.3 4.7 %copy-start.14 = (f32[2,128]{1,0:T(2,128)S(1)}, f32[2,128]{1,0:T(2,128)}, u32[]{:S(2)}) copy-start(f32[2,128]{1,0:T(2,128)} %param.26) | copy-start | bytes 3076
  28.4 4.7 %copy-start.6 = (bf16[384,128]{1,0:T(8,128)(2,1)S(1)}, bf16[384,128]{1,0:T(8,128)(2,1)}, u32[]{:S(2)}) copy-start(bf16[384,128]{1,0:T(8,128)(2,1)} %param.18) | copy-start | bytes 294916
  28.4 4.7 %copy-start.16 = (bf16[2,128,128]{2,1,0:T(8,128)(2,1)S(1)}, bf16[2,128,128]{2,1,0:T(8,128)(2,1)}, u32[]{:S(2)}) copy-start(bf16[2,128,128]{2,1,0:T(8,128)(2,1)} %param.25) | copy-start | bytes 196612
  43.3 2.1 %copy-start.4 = (f32[12,4,32,128]{3,2,1,0:T(8,128)S(1)}, f32[12,4,32,128]{3,2,1,0:T(8,128)}, u32[]{:S(2)}) copy-start(f32[12,4,32,128]{3,2,1,0:T(8,128)} %copy.44) | copy-start | bytes 2359300
  45.4 3.1 %copy-start.5 = (bf16[4,12,128,128]{2,3,1,0:T(8,128)(2,1)S(1)}, bf16[4,12,128,128]{2,3,1,0:T(8,128)(2,1)}, u32[]{:S(2)}) copy-start(bf16[4,12,128,128]{2,3,1,0:T(8,128)(2,1)} %copy.41) | copy-start | bytes 4718596
  56.3 2.2 %copy-start.7 = (f32[384,128]{0,1:T(8,128)S(1)}, f32[384,128]{0,1:T(8,128)}, u32[]{:S(2)}) copy-start(f32[384,128]{0,1:T(8,128)} %copy.48) | copy-start | bytes 589828
  56.3 2.2 %copy-start.10 = (bf16[128,512]{1,0:T(8,128)(2,1)S(1)}, bf16[128,512]{1,0:T(8,128)(2,1)}, u32[]{:S(2)}) copy-start(bf16[128,512]{1,0:T(8,128)(2,1)} %param.31) | copy-start | bytes 393220
  58.4 0.9 %copy-start.8 = (f32[384,128]{0,1:T(8,128)S(1)}, f32[384,128]{0,1:T(8,128)}, u32[]{:S(2)}) copy-start(f32[384,128]{0,1:T(8,128)} %copy.47) | copy-start | bytes 589828
  58.4 0.9 %copy-start.17 = (bf16[256,128]{1,0:T(8,128)(2,1)S(1)}, bf16[256,128]{1,0:T(8,128)(2,1)}, u32[]{:S(2)}) copy-start(bf16[256,128]{1,0:T(8,128)(2,1)} %param.32) | copy-start | bytes 196612
  59.3 0.7 copy-start.18
  61.4 3.1 %collective-permute-start.4 = (f32[4,1,768]{2,1,0:T(1,128)S(1)}, f32[4,1,768]{2,1,0:T(1,128)S(1)}, u32[]{:S(2)}, u32[]{:S(2)}) collective-permute-start(f32[4,1,768]{2,1,0:T(1,128)S(1)} %slice.190), channel_id=1, source_target_pairs={{0,1},{1,2},{2,3},{3,4},{4,5},{5,6},{6,7},{7,8},{8,9},{9,10},{10,1... | collective-permute-start | bytes 36872 | tf_op jit(solution)/shard_map/ppermute | solution.py:19
  64.5 7.3 %collective-permute-start.5 = (f32[4,1,768]{2,1,0:T(1,128)S(1)}, f32[4,1,768]{2,1,0:T(1,128)S(1)}, u32[]{:S(2)}, u32[]{:S(2)}) collective-permute-start(f32[4,1,768]{2,1,0:T(1,128)S(1)} %get-tuple-element.15), channel_id=1, source_target_pairs={{1,0},{2,1},{3,2},{4,3},{5,4},{6,5},{7,6},{8,7},{9,8},{10,9},{11,1... | collective-permute-start | bytes 36872 | tf_op jit(solution)/shard_map/ppermute | solution.py:20
where the time goes:
time: 73.3 us; the launch traced here: 72.7 us
  local copies, waits for them, and re-layouts  19.6 us (27%)
  starting transfers between devices  19.6 us (27%)
  matrix products  14.7 us (20%)
  other arithmetic  11.6 us (16%)
  waiting for transfers between devices  5.24 us (7%)
  between operations  1.9 us (3%)
    ppermute x3, starting transfers between devices, extended_2(): before = lax.ppermute(last, axis, up)  12.8 us
    ppermute x3, starting transfers between devices, extended_2(): after = lax.ppermute(initial, axis, down)  6.81 us
    ppermute x3, waiting for transfers between devices, extended_2(): after = lax.ppermute(initial, axis, down)  4.22 us
    transpose x1, local copies, waits for them, and re-layouts, on_device(): jnp.einsum('bwhij,bwjhd->bwihd', attention, values_win, preferred_element...  3.28 us
    sub x1, other arithmetic, on_device(): attention = jax.nn.softmax(scores, axis=-1).astype(jnp.bfloat16)  3.04 us
    div x4, local copies, waits for them, and re-layouts, on_device(): jax.nn.sigmoid(jnp.dot(cond_norm, zero_weight[which], preferred_element_t...  2.59 us
    dot_general x1, matrix products, on_device(): jnp.einsum('bwhij,bwjhd->bwihd', attention, values_win, preferred_element...  2.42 us
    unnamed x40, local copies, waits for them, and re-layouts  2.38 us
  transfers between devices with their start and end apart: 6, of which 2 were waited for; matrix products, arithmetic and copies ran while one was open for 18% of the time, Pallas kernels for 0%

commit v1 on v0

v1 whole, which is shorter than its diff:
```python
import functools

import jax
import jax.numpy as jnp
from jax import lax
from jax.experimental import pallas as pl
from jax.experimental.pallas import tpu as pltpu
from jax.sharding import PartitionSpec as P

ATOMS_PER_TOKEN = 8
EPS = 1e-05
HALO = 80
EDGE = 16
EDGE_Q = 8
MASKED = -1e30
BF16 = jnp.bfloat16
F32 = jnp.float32


def dot(a, b):
    return jnp.dot(a, b, preferred_element_type=F32)


def dot_t(a, b):
    return lax.dot_general(a, b, (((1,), (1,)), ((), ())), preferred_element_type=F32)


def norm_rows(x):
    center = jnp.mean(x, -1, keepdims=True)
    off = x - center
    spread = jnp.mean(jnp.square(off), -1, keepdims=True)
    return off * lax.rsqrt(spread + EPS)


def sigmoid(x):
    return 1.0 / (1.0 + jnp.exp(-x))


def iota(shape, dim):
    return lax.broadcasted_iota(jnp.int32, shape, dim)


def pack_kernel(
    count_ref, mask_ref, token_ref, atoms_ref, cond_ref, pair_ref, up_ref, down_ref, info_ref, sems
):
    samples, atom_dev, _ = atoms_ref.shape
    channels = pair_ref.shape[2]
    windows, query_len = pair_ref.shape[:2]
    copies = []

    def copy(src, dst):
        c = pltpu.make_async_copy(src, dst, sems.at[len(copies)])
        c.start()
        copies.append(c)

    for wire, at in ((up_ref, atom_dev - HALO), (down_ref, 0)):
        for s in range(samples):
            copy(atoms_ref.at[s, pl.ds(at, HALO)], wire.at[pl.ds(s * HALO, HALO)])
        copy(cond_ref.at[pl.ds(at, HALO)], wire.at[pl.ds(samples * HALO, HALO)])
    rows = (samples + 1) * HALO
    for wire, w, i in ((up_ref, windows - 1, query_len - EDGE_Q), (down_ref, 0, 0)):
        for q in range(EDGE_Q):
            copy(pair_ref.at[w, i + q], wire.at[pl.ds(rows + q * channels, channels)])
    rows += EDGE_Q * channels
    device = lax.axis_index("atom")
    position = device * atom_dev + iota((1, atom_dev), 1)
    usable = jnp.where((mask_ref[...] == 1) & (position < count_ref[0]), 1.0, 0.0)
    own = (token_ref[...] - device * (atom_dev // ATOMS_PER_TOKEN)).astype(F32)
    for slot, at in ((0, atom_dev - 128), (1, 0)):
        flags = usable[:, at : at + 128]
        tokens = own[:, at : at + 128]
        row = iota((16, 128), 0)
        block = jnp.where(row == 0, flags, jnp.where(row == 1, tokens, 0.0))
        info_ref[slot] = block.astype(BF16)
    copy(info_ref.at[0], up_ref.at[pl.ds(rows, 16)])
    copy(info_ref.at[1], down_ref.at[pl.ds(rows, 16)])
    for c in copies:
        c.wait()


def pair_lhs(weight_ref, lhs_ref):
    heads, channels = weight_ref.shape
    wide = 16 * channels
    w = weight_ref[...]
    w = w - jnp.mean(w, -1, keepdims=True)
    spread = jnp.where(iota((channels, wide), 1) % channels == iota((channels, wide), 0), 1.0, 0.0)
    tiled = jnp.dot(w, spread, precision=lax.Precision.HIGHEST, preferred_element_type=F32)
    full = jnp.concatenate(
        [jnp.broadcast_to(tiled[h : h + 1], (16, wide)) for h in range(heads)], axis=0
    )
    shape = (16 * heads, wide)
    full = jnp.where(iota(shape, 1) // channels == iota(shape, 0) % 16, full, 0.0)
    high = full.astype(BF16)
    rest = full - high.astype(F32)
    mid = rest.astype(BF16)
    low = (rest - mid.astype(F32)).astype(BF16)
    shape = (wide, wide)
    mean = jnp.where(iota(shape, 0) // channels == iota(shape, 1) // channels, 1.0 / channels, 0.0)
    n = 16 * heads
    lhs_ref[0:wide] = mean.astype(BF16)
    lhs_ref[wide : wide + n] = high
    lhs_ref[wide + n : wide + 2 * n] = mid
    lhs_ref[wide + 2 * n : wide + 3 * n] = low


def pair_bias(x, lhs, queries, heads):
    rows = queries * 16
    n = 16 * heads
    keys = x.shape[1]
    out = dot(lhs, x)
    off = x.astype(F32) - out[0:256][:rows]
    square = off * off
    half = jnp.sum(square.reshape(queries, 2, 8, keys), axis=1).reshape(queries * 8, keys)
    shape = (queries, queries * 8)
    gather = jnp.where(iota(shape, 1) // 8 == iota(shape, 0), 1.0 / 16, 0.0).astype(BF16)
    high = half.astype(BF16)
    low = (half - high.astype(F32)).astype(BF16)
    spread = dot(gather, high) + dot(gather, low)
    rstd = lax.rsqrt(spread + EPS)
    sums = out[256 : 256 + n] + out[256 + n : 256 + 2 * n] + out[256 + 2 * n : 256 + 3 * n]
    return [sums[h * 16 : h * 16 + queries] * rstd for h in range(heads)]


def bias_kernel(weight_ref, pair_ref, bias_ref, lhs_out_ref, lhs_ref):
    heads = weight_ref.shape[0]

    @pl.when(pl.program_id(0) == 0)
    def _():
        pair_lhs(weight_ref, lhs_ref)
        lhs_out_ref[...] = lhs_ref[...]

    lhs = lhs_ref[...]
    for w in range(pair_ref.shape[0]):
        query_len = pair_ref.shape[1] // 16
        for c in range(query_len // 16):
            x = pair_ref[w, c * 256 : (c + 1) * 256]
            for h, b in enumerate(pair_bias(x, lhs, 16, heads)):
                bias_ref[w, h * query_len + c * 16 : h * query_len + c * 16 + 16] = b


def block_kernel(
    count_ref,
    mask_ref,
    token_ref,
    atoms_ref,
    cond_ref,
    left_ref,
    right_ref,
    bias_ref,
    lhs_ref,
    ada_w_ref,
    ada_b_ref,
    zero_w_ref,
    zero_b_ref,
    qkvg_ref,
    query_b_ref,
    out_w_ref,
    swiglu_ref,
    down_ref,
    token_w_ref,
    atoms_out_ref,
    tokens_out_ref,
    scale0,
    shift0,
    scale1,
    shift1,
    gate0,
    gate1,
    edge_bias,
    live_ref,
    onehot_ref,
    inverse_ref,
    q_ref,
    k_ref,
    v_ref,
    gate_ref,
    blend_ref,
):
    atom_dev, width = atoms_ref.shape[1:]
    windows, score_rows, key_len = bias_ref.shape
    query_len = atom_dev // windows
    heads = score_rows // query_len
    head_dim = width // heads
    margin = (key_len - query_len) // 2
    tok_dev = atom_dev // ATOMS_PER_TOKEN
    samples = pl.num_programs(0)
    sample = pl.program_id(0)
    ext = atom_dev + 2 * HALO
    rows = atom_dev + 2 * EDGE
    first = HALO - EDGE
    hidden = down_ref.shape[0]

    @pl.when(sample == 0)
    def _():
        at = 4 * HALO
        cond = jnp.concatenate(
            [left_ref[at : at + HALO], cond_ref[...], right_ref[at : at + HALO]], axis=0
        )
        norm = norm_rows(cond.astype(F32)).astype(BF16)
        adapt = dot(norm, ada_w_ref[0])
        scale0[...] = sigmoid(adapt[:, :width] + ada_b_ref[0:1])
        shift0[...] = adapt[:, width:]
        norm = norm[first : first + rows]
        adapt = dot(norm, ada_w_ref[1])
        scale1[...] = sigmoid(adapt[:, :width] + ada_b_ref[1:2])
        shift1[...] = adapt[:, width:]
        gate0[...] = sigmoid(dot(norm, zero_w_ref[0]) + zero_b_ref[0:1])
        gate1[...] = sigmoid(dot(norm, zero_w_ref[1]) + zero_b_ref[1:2])
        at += HALO
        for e, ref in enumerate((left_ref, right_ref)):
            x = ref[at : at + EDGE_Q * 16]
            x = jnp.concatenate([x, jnp.zeros_like(x)], axis=0)
            for h, b in enumerate(pair_bias(x, lhs_ref[...], 16, heads)):
                edge_bias[e, h * EDGE_Q : (h + 1) * EDGE_Q] = b[:EDGE_Q]
        at += EDGE_Q * 16
        device = lax.axis_index("atom")
        position = device * atom_dev + iota((1, atom_dev), 1)
        usable = jnp.where((mask_ref[...] == 1) & (position < count_ref[0]), 1.0, 0.0)
        own = (token_ref[...] - device * tok_dev).astype(F32)
        info_l = left_ref[at : at + 16].astype(F32)
        info_r = right_ref[at : at + 16].astype(F32)
        flags = jnp.concatenate([info_l[0:1], usable, info_r[0:1]], axis=1)
        tokens = jnp.concatenate(
            [info_l[1:2] - tok_dev, own, info_r[1:2] + tok_dev], axis=1
        )
        total = flags.shape[1]
        flags8 = jnp.broadcast_to(flags, (8, total))
        rolled = {}
        for w in range(-1, windows + 1):
            start = 128 + query_len * w - margin
            shift = start % 128
            if shift not in rolled:
                rolled[shift] = pltpu.roll(flags8, total - shift, 1)
            lane = start - shift
            row = rolled[shift][0:1, lane : lane + key_len]
            live_ref[w + 1 : w + 2] = jnp.where(row > 0.5, 0.0, MASKED)
        shift = 128 - EDGE
        flags = pltpu.roll(flags8, total - shift, 1)[0:1]
        tokens = pltpu.roll(jnp.broadcast_to(tokens, (8, total)), total - shift, 1)[0:1]
        lanes = onehot_ref.shape[1]
        slot = iota((tok_dev, lanes), 0).astype(F32)
        inside = iota((tok_dev, lanes), 1) < rows
        hit = (tokens[:, :lanes] == slot) & (flags[:, :lanes] > 0.5) & inside
        onehot = jnp.where(hit, 1.0, 0.0)
        onehot_ref[...] = onehot.astype(BF16)
        counts = jnp.sum(onehot, -1, keepdims=True)
        inverse_ref[...] = jnp.broadcast_to(1.0 / jnp.maximum(counts, 1.0), inverse_ref.shape)
        v_ref[:, width:] = jnp.ones((ext, width), BF16)

    at = pl.multiple_of(sample * HALO, 16)
    stream = jnp.concatenate(
        [left_ref[pl.ds(at, HALO)], atoms_ref[0], right_ref[pl.ds(at, HALO)]], axis=0
    ).astype(F32)
    attn_in = (norm_rows(stream) * scale0[...] + shift0[...]).astype(BF16)
    keyval = dot(attn_in, qkvg_ref[:, width : 3 * width])
    k_ref[...] = keyval[:, :width].astype(BF16)
    v_ref[:, :width] = keyval[:, width:].astype(BF16)
    inner = attn_in[first : first + rows]
    factor = head_dim ** (-0.5)
    queries = dot(inner, qkvg_ref[:, :width])
    q_ref[...] = (queries + query_b_ref[0:1]) * factor
    gate_ref[...] = sigmoid(dot(inner, qkvg_ref[:, 3 * width :]))

    lane_head = iota((1, width), 1) // head_dim

    def attend(q, keys_at, bias, live):
        n = q.shape[0]
        wide = jnp.concatenate(
            [jnp.where(lane_head == h, q, 0.0) for h in range(heads)], axis=0
        ).astype(BF16)
        scores = dot_t(wide, k_ref[keys_at : keys_at + key_len]) + (bias + live)
        top = jnp.max(scores, -1, keepdims=True)
        weights = jnp.exp(scores - top).astype(BF16)
        out = dot(weights, v_ref[keys_at : keys_at + key_len])
        pick = out[0:n]
        for h in range(1, heads):
            head = jnp.concatenate([lane_head, lane_head], axis=1)
            pick = jnp.where(head == h, out[h * n : (h + 1) * n], pick)
        return pick[:, :width] / pick[:, width:]

    for w in range(windows):
        r = EDGE + w * query_len
        got = attend(
            q_ref[r : r + query_len],
            HALO + w * query_len - margin,
            bias_ref[w],
            live_ref[w + 1 : w + 2],
        )
        blend_ref[r : r + query_len] = (got * gate_ref[r : r + query_len]).astype(BF16)
    for e in range(2):
        r = (EDGE - EDGE_Q, EDGE + atom_dev)[e]
        w = (-1, windows)[e]
        got = attend(
            q_ref[r : r + EDGE_Q],
            HALO + w * query_len - margin,
            edge_bias[e],
            live_ref[w + 1 : w + 2],
        )
        got = got * gate_ref[r : r + EDGE_Q]
        pad = jnp.zeros_like(got)
        both = jnp.concatenate([pad, got] if e == 0 else [got, pad], axis=0)
        b = (0, EDGE + atom_dev)[e]
        blend_ref[b : b + EDGE] = both.astype(BF16)

    after = (
        stream[first : first + rows] + gate0[...] * dot(blend_ref[...], out_w_ref[...])
    ).astype(BF16)
    after32 = after.astype(F32)
    trans_in = (norm_rows(after32) * scale1[...] + shift1[...]).astype(BF16)
    mixed = dot(trans_in, swiglu_ref[...])
    a = mixed[:, :hidden]
    units = (a * sigmoid(a) * mixed[:, hidden:]).astype(BF16)
    result = (after32 + gate1[...] * dot(units, down_ref[...])).astype(BF16)
    atoms_out_ref[0] = result[EDGE : EDGE + atom_dev]
    features = jnp.maximum(dot(result, token_w_ref[...]), 0.0).astype(BF16)
    totals = dot(onehot_ref[:, :rows], features)
    for c in range(0, totals.shape[1], 128):
        tokens_out_ref[0, :, c : c + 128] = (totals[:, c : c + 128] * inverse_ref[...]).astype(
            BF16
        )


def on_device(
    atoms_in,
    cond,
    pair,
    atom_mask,
    atom_count,
    atom_to_token,
    ada_weight,
    ada_bias,
    zero_weight,
    zero_bias,
    qkvg_weight,
    query_bias,
    pair_weight,
    out_weight,
    swiglu_weight,
    down_weight,
    token_weight,
):
    samples, atom_dev, width = atoms_in.shape
    windows, query_len, channels, key_len = pair.shape
    heads = pair_weight.shape[0]
    hidden = down_weight.shape[0]
    token_width = token_weight.shape[1]
    tok_dev = atom_dev // ATOMS_PER_TOKEN
    ext = atom_dev + 2 * HALO
    rows = atom_dev + 2 * EDGE
    mask = atom_mask.reshape(1, atom_dev)
    token = atom_to_token.reshape(1, atom_dev)
    smem = pl.BlockSpec(memory_space=pltpu.SMEM)
    anywhere = pl.BlockSpec(memory_space=pl.ANY)
    vmem = pl.BlockSpec(memory_space=pltpu.VMEM)

    wire_rows = (samples + 1) * HALO + EDGE_Q * channels + 16
    wire = jax.ShapeDtypeStruct((wire_rows, width), BF16)
    n_copies = 2 * (samples + 1 + EDGE_Q + 1)
    up, down = pl.pallas_call(
        pack_kernel,
        out_shape=(wire, wire),
        in_specs=[smem, vmem, vmem, anywhere, anywhere, anywhere],
        out_specs=(anywhere, anywhere),
        scratch_shapes=[pltpu.VMEM((2, 16, 128), BF16), pltpu.SemaphoreType.DMA((n_copies,))],
        name="pack",
    )(atom_count, mask, token, atoms_in, cond, pair)
    count = lax.axis_size("atom")
    to_right = [(i, i + 1) for i in range(count - 1)]
    to_left = [(i + 1, i) for i in range(count - 1)]
    left = lax.ppermute(up, "atom", to_right)
    right = lax.ppermute(down, "atom", to_left)

    lhs_shape = (16 * channels + 3 * 16 * heads, 16 * channels)
    per_step = 3
    bias, lhs = pl.pallas_call(
        bias_kernel,
        grid=(windows // per_step,),
        out_shape=(
            jax.ShapeDtypeStruct((windows, heads * query_len, key_len), F32),
            jax.ShapeDtypeStruct(lhs_shape, BF16),
        ),
        in_specs=[
            pl.BlockSpec((heads, channels), lambda i: (0, 0)),
            pl.BlockSpec((per_step, query_len * channels, key_len), lambda i: (i, 0, 0)),
        ],
        out_specs=(
            pl.BlockSpec((per_step, heads * query_len, key_len), lambda i: (i, 0, 0)),
            pl.BlockSpec(lhs_shape, lambda i: (0, 0)),
        ),
        scratch_shapes=[pltpu.VMEM(lhs_shape, BF16)],
        name="bias",
    )(pair_weight, pair.reshape(windows, query_len * channels, key_len))

    def whole(array):
        zeros = (0,) * array.ndim
        return pl.BlockSpec(array.shape, lambda s: zeros)

    weights = (
        ada_weight,
        ada_bias,
        zero_weight,
        zero_bias,
        qkvg_weight,
        query_bias.reshape(1, width),
        out_weight,
        swiglu_weight,
        down_weight,
        token_weight,
    )
    resident = (cond, left, right, bias, lhs) + weights
    return pl.pallas_call(
        block_kernel,
        grid=(samples,),
        out_shape=(
            jax.ShapeDtypeStruct((samples, atom_dev, width), BF16),
            jax.ShapeDtypeStruct((samples, tok_dev, token_width), BF16),
        ),
        in_specs=[
            smem,
            whole(mask),
            whole(token),
            pl.BlockSpec((1, atom_dev, width), lambda s: (s, 0, 0)),
        ]
        + [whole(a) for a in resident],
        out_specs=(
            pl.BlockSpec((1, atom_dev, width), lambda s: (s, 0, 0)),
            pl.BlockSpec((1, tok_dev, token_width), lambda s: (s, 0, 0)),
        ),
        scratch_shapes=[
            pltpu.VMEM((ext, width), F32),
            pltpu.VMEM((ext, width), F32),
            pltpu.VMEM((rows, width), F32),
            pltpu.VMEM((rows, width), F32),
            pltpu.VMEM((rows, width), F32),
            pltpu.VMEM((rows, width), F32),
            pltpu.VMEM((2, heads * EDGE_Q, key_len), F32),
            pltpu.VMEM((16, key_len), F32),
            pltpu.VMEM((tok_dev, 512), BF16),
            pltpu.VMEM((tok_dev, 128), F32),
            pltpu.VMEM((rows, width), F32),
            pltpu.VMEM((ext, width), BF16),
            pltpu.VMEM((ext, 2 * width), BF16),
            pltpu.VMEM((rows, width), F32),
            pltpu.VMEM((rows, width), BF16),
        ],
        compiler_params=pltpu.CompilerParams(dimension_semantics=("arbitrary",)),
        name="block",
    )(atom_count, mask, token, atoms_in, *resident)


def solution(mesh):
    in_specs = (
        P("struct", "atom", None),
        P(("struct", "atom"), None),
        P(("struct", "atom"), None, None, None),
        P(("struct", "atom")),
        P("struct"),
        P(("struct", "atom")),
        P(),
        P(),
        P(),
        P(),
        P(),
        P(),
        P(),
        P(),
        P(),
        P(),
        P(),
    )
    out_specs = (P("struct", "atom", None), P("struct", "atom", None))
    return jax.shard_map(
        on_device, mesh=mesh, in_specs=in_specs, out_specs=out_specs, check_vma=False
    )
```

time: 73.3 us -> 46.7 us (0.64)
  the two profiles are of different devices: /device:TPU:189 before, /device:TPU:98 now
where the time goes in v1:
time: 46.7 us; the launch traced here: 46.4 us
  Pallas kernels  34.2 us (73%)
  starting transfers between devices  7.67 us (16%)
  local copies, waits for them, and re-layouts  3.22 us (7%)
  between operations  1.32 us (3%)
    pallas_call x1, Pallas kernels, on_device(): pl.pallas_call(block_kernel, grid=(samples,), out_shape=(jax.ShapeDtypeSt...  16.7 us
    pallas_call x1, Pallas kernels, on_device(): pl.pallas_call(pack_kernel, out_shape=(wire, wire), in_specs=[smem, vmem,...  10.2 us
    pallas_call x1, Pallas kernels, on_device(): pl.pallas_call(bias_kernel, grid=(windows // per_step,), out_shape=(jax.S...  7.22 us
    ppermute x1, starting transfers between devices, on_device(): right = lax.ppermute(down, 'atom', to_left)  5.75 us
    ppermute x1, starting transfers between devices, on_device(): left = lax.ppermute(up, 'atom', to_right)  1.92 us
    reshape x1, local copies, waits for them, and re-layouts, on_device(): mask = atom_mask.reshape(1, atom_dev)  1.28 us
    reshape x1, local copies, waits for them, and re-layouts, on_device(): token = atom_to_token.reshape(1, atom_dev)  1.26 us
  transfers between devices with their start and end apart: 2, of which 0 were waited for; matrix products, arithmetic and copies ran while one was open for 0% of the time, Pallas kernels for 16%

profile of v1, /device:TPU:98, one launch (start us, length us, event | category | flops | bytes accessed | tf_op | source)
XLA Modules:
  0.0 46.4 jit_solution(10508670132152425149)
XLA Ops:
  1.3 1.3 %reshape.16.mask_ref = s32[1,384]{1,0:T(1,128)} reshape(s32[384]{0:T(512)} %param.20) | data formatting | bytes 3072 | tf_op jit(solution)/shard_map/reshape | solution.py:350
  2.6 1.3 %reshape.17.token_ref = s32[1,384]{1,0:T(1,128)} reshape(s32[384]{0:T(512)} %param.22) | data formatting | bytes 3072 | tf_op jit(solution)/shard_map/reshape | solution.py:351
  3.8 10.2 %pack.1 = (bf16[544,128]{1,0:T(8,128)(2,1)}, bf16[544,128]{1,0:T(8,128)(2,1)}) custom-call(s32[1]{0:T(128)S(6)} %copy.19.count_ref, s32[1,384]{1,0:T(1,128)} %reshape.16.mask_ref, s32[1,384]{1,0:T(1,128)} %reshape.17.token_ref, bf16[4,384,128]{2,1,0:T(8,128)(2,1)} %atoms_ref.3, bf16[384,128]{1,0:T(8,128)(2,1)} %cond_ref.3, bf16[12,32,16,128]{3,2,1,0:T(8,128)(2,1)} %pair_ref.1), custom_call_target="tpu_custom_call" | custom-call | tf_op jit(solution)/shard_map/pack/pallas_call | solution.py:359
  14.0 1.9 %collective-permute-start = (bf16[544,128]{1,0:T(8,128)(2,1)}, bf16[544,128]{1,0:T(8,128)(2,1)S(1)}, u32[]{:S(2)}, u32[]{:S(2)}) collective-permute-start(bf16[544,128]{1,0:T(8,128)(2,1)} %get-tuple-element.6), channel_id=1, source_target_pairs={{0,1},{1,2},{2,3},{3,4},{4,5},{5,6},{6,7},{7,8},{8,9},{9,10},{10,1... | collective-permute-start | bytes 417800 | tf_op jit(solution)/shard_map/ppermute | solution.py:370
  16.0 5.8 %collective-permute-start.1 = (bf16[544,128]{1,0:T(8,128)(2,1)}, bf16[544,128]{1,0:T(8,128)(2,1)S(1)}, u32[]{:S(2)}, u32[]{:S(2)}) collective-permute-start(bf16[544,128]{1,0:T(8,128)(2,1)} %get-tuple-element.7), channel_id=1, source_target_pairs={{1,0},{2,1},{3,2},{4,3},{5,4},{6,5},{7,6},{8,7},{9,8},{10,9},{11,1... | collective-permute-start | bytes 417800 | tf_op jit(solution)/shard_map/ppermute | solution.py:371
  21.7 7.2 %bias.1 = (f32[12,128,128]{2,1,0:T(8,128)}, bf16[448,256]{1,0:T(8,128)(2,1)}) custom-call(f32[4,16]{1,0:T(4,128)} %weight_ref.1, bf16[12,512,128]{2,1,0:T(8,128)(2,1)} %bitcast.2), custom_call_target="tpu_custom_call" | custom-call | tf_op jit(solution)/shard_map/bias/pallas_call | solution.py:375
  29.0 0.0 collective-permute-done.left_ref
  29.0 0.0 copy-start
  29.0 0.0 collective-permute-done.1.right_ref
  29.0 0.0 copy-start.1
  29.0 0.6 %copy-done = bf16[544,128]{1,0:T(8,128)(2,1)} copy-done((bf16[544,128]{1,0:T(8,128)(2,1)}, bf16[544,128]{1,0:T(8,128)(2,1)S(1)}, u32[]{:S(2)}) %copy-start) | copy-done | bytes 139288
  29.6 0.0 copy-done.1
  29.7 16.7 %block.1 = (bf16[4,384,128]{2,1,0:T(8,128)(2,1)}, bf16[4,48,768]{2,1,0:T(8,128)(2,1)}) custom-call(s32[1]{0:T(128)S(6)} %copy.19.count_ref, s32[1,384]{1,0:T(1,128)} %reshape.16.mask_ref, s32[1,384]{1,0:T(1,128)} %reshape.17.token_ref, bf16[4,384,128]{2,1,0:T(8,128)(2,1)} %atoms_ref.3, bf16[384,128]{1,0:T(8,128)(2,1)} %cond_ref.3, bf16[544,128]{1,0:T(8,128)(2,1)} %copy-done, ...), custom_call_target="tpu_custom_call" | custom-call | tf_op jit(solution)/shard_map/block/pallas_call | solution.py:411
Async XLA Ops:
  14.0 14.9 %collective-permute-start = (bf16[544,128]{1,0:T(8,128)(2,1)}, bf16[544,128]{1,0:T(8,128)(2,1)S(1)}, u32[]{:S(2)}, u32[]{:S(2)}) collective-permute-start(bf16[544,128]{1,0:T(8,128)(2,1)} %get-tuple-element.6), channel_id=1, source_target_pairs={{0,1},{1,2},{2,3},{3,4},{4,5},{5,6},{6,7},{7,8},{8,9},{9,10},{10,1... | collective-permute-start | bytes 417800 | tf_op jit(solution)/shard_map/ppermute | solution.py:370
  16.0 13.0 %collective-permute-start.1 = (bf16[544,128]{1,0:T(8,128)(2,1)}, bf16[544,128]{1,0:T(8,128)(2,1)S(1)}, u32[]{:S(2)}, u32[]{:S(2)}) collective-permute-start(bf16[544,128]{1,0:T(8,128)(2,1)} %get-tuple-element.7), channel_id=1, source_target_pairs={{1,0},{2,1},{3,2},{4,3},{5,4},{6,5},{7,6},{8,7},{9,8},{10,9},{11,1... | collective-permute-start | bytes 417800 | tf_op jit(solution)/shard_map/ppermute | solution.py:371
  29.0 0.7 %copy-start = (bf16[544,128]{1,0:T(8,128)(2,1)}, bf16[544,128]{1,0:T(8,128)(2,1)S(1)}, u32[]{:S(2)}) copy-start(bf16[544,128]{1,0:T(8,128)(2,1)S(1)} %collective-permute-done.left_ref) | copy-start | bytes 417796
  29.0 0.7 %copy-start.1 = (bf16[544,128]{1,0:T(8,128)(2,1)}, bf16[544,128]{1,0:T(8,128)(2,1)S(1)}, u32[]{:S(2)}) copy-start(bf16[544,128]{1,0:T(8,128)(2,1)S(1)} %collective-permute-done.1.right_ref) | copy-start | bytes 417796

commit v2 on v1

v2 whole, which is shorter than its diff:
```python
import functools

import jax
import jax.numpy as jnp
from jax import lax
from jax.experimental import pallas as pl
from jax.experimental.pallas import tpu as pltpu
from jax.sharding import PartitionSpec as P

ATOMS_PER_TOKEN = 8
EPS = 1e-05
HALO = 80
EDGE = 16
EDGE_Q = 8
MASKED = -1e30
BF16 = jnp.bfloat16
F32 = jnp.float32


def dot(a, b):
    return jnp.dot(a, b, preferred_element_type=F32)


def dot_t(a, b):
    return lax.dot_general(a, b, (((1,), (1,)), ((), ())), preferred_element_type=F32)


def norm_rows(x):
    center = jnp.mean(x, -1, keepdims=True)
    off = x - center
    spread = jnp.mean(jnp.square(off), -1, keepdims=True)
    return off * lax.rsqrt(spread + EPS)


def sigmoid(x):
    return 1.0 / (1.0 + jnp.exp(-x))


def iota(shape, dim):
    return lax.broadcasted_iota(jnp.int32, shape, dim)


def pack_kernel(
    count_ref,
    mask_hbm,
    token_hbm,
    atoms_ref,
    cond_ref,
    pair_ref,
    up_ref,
    down_ref,
    info_ref,
    mask_ref,
    token_ref,
    sems,
):
    samples, atom_dev, _ = atoms_ref.shape
    windows, pair_rows, _ = pair_ref.shape
    edge_rows = EDGE_Q * 16
    copies = []

    def copy(src, dst):
        c = pltpu.make_async_copy(src, dst, sems.at[len(copies)])
        c.start()
        copies.append(c)

    copy(mask_hbm, mask_ref)
    copy(token_hbm, token_ref)
    rows = (samples + 1) * HALO
    for wire, at, w, p in (
        (up_ref, atom_dev - HALO, windows - 1, pair_rows - edge_rows),
        (down_ref, 0, 0, 0),
    ):
        for s in range(samples):
            copy(atoms_ref.at[s, pl.ds(at, HALO)], wire.at[pl.ds(s * HALO, HALO)])
        copy(cond_ref.at[pl.ds(at, HALO)], wire.at[pl.ds(samples * HALO, HALO)])
        copy(pair_ref.at[w, pl.ds(p, edge_rows)], wire.at[pl.ds(rows, edge_rows)])
    rows += edge_rows
    device = lax.axis_index("atom")
    position = device * atom_dev + iota((1, atom_dev), 1)
    for c in copies[:2]:
        c.wait()
    mask = mask_ref[...].reshape(1, atom_dev)
    token = token_ref[...].reshape(1, atom_dev)
    usable = jnp.where((mask == 1) & (position < count_ref[0]), 1.0, 0.0)
    own = (token - device * (atom_dev // ATOMS_PER_TOKEN)).astype(F32)
    row = iota((16, atom_dev), 0)
    info = jnp.where(row == 0, usable, jnp.where(row == 1, own, 0.0))
    info_ref[...] = info
    up_ref[rows : rows + 16] = info[:, atom_dev - 128 :].astype(BF16)
    down_ref[rows : rows + 16] = info[:, :128].astype(BF16)
    for c in copies[2:]:
        c.wait()


def pair_lhs(weight_ref, lhs_ref):
    heads, channels = weight_ref.shape
    wide = 16 * channels
    w = weight_ref[...]
    w = w - jnp.mean(w, -1, keepdims=True)
    spread = jnp.where(iota((channels, wide), 1) % channels == iota((channels, wide), 0), 1.0, 0.0)
    tiled = jnp.dot(w, spread, precision=lax.Precision.HIGHEST, preferred_element_type=F32)
    full = jnp.concatenate(
        [jnp.broadcast_to(tiled[h : h + 1], (16, wide)) for h in range(heads)], axis=0
    )
    shape = (16 * heads, wide)
    full = jnp.where(iota(shape, 1) // channels == iota(shape, 0) % 16, full, 0.0)
    high = full.astype(BF16)
    rest = full - high.astype(F32)
    mid = rest.astype(BF16)
    low = (rest - mid.astype(F32)).astype(BF16)
    shape = (wide, wide)
    mean = jnp.where(iota(shape, 0) // channels == iota(shape, 1) // channels, 1.0 / channels, 0.0)
    n = 16 * heads
    lhs_ref[0:wide] = mean.astype(BF16)
    lhs_ref[wide : wide + n] = high
    lhs_ref[wide + n : wide + 2 * n] = mid
    lhs_ref[wide + 2 * n : wide + 3 * n] = low


def pair_bias(x, lhs, queries, heads):
    rows = queries * 16
    n = 16 * heads
    keys = x.shape[1]
    out = dot(lhs, x)
    off = x.astype(F32) - out[0:256][:rows]
    square = off * off
    half = jnp.sum(square.reshape(queries, 2, 8, keys), axis=1).reshape(queries * 8, keys)
    shape = (queries, queries * 8)
    gather = jnp.where(iota(shape, 1) // 8 == iota(shape, 0), 1.0 / 16, 0.0).astype(BF16)
    high = half.astype(BF16)
    low = (half - high.astype(F32)).astype(BF16)
    spread = dot(gather, high) + dot(gather, low)
    rstd = lax.rsqrt(spread + EPS)
    sums = out[256 : 256 + n] + out[256 + n : 256 + 2 * n] + out[256 + 2 * n : 256 + 3 * n]
    return [sums[h * 16 : h * 16 + queries] * rstd for h in range(heads)]


def bias_kernel(weight_ref, pair_ref, bias_ref, lhs_ref):
    heads = weight_ref.shape[0]
    pair_lhs(weight_ref, lhs_ref)
    query_len = pair_ref.shape[1] // 16

    def window(w, carry):
        for c in range(query_len // 16):
            x = pair_ref[w, c * 256 : (c + 1) * 256]
            for h, b in enumerate(pair_bias(x, lhs_ref[...], 16, heads)):
                bias_ref[w, h * query_len + c * 16 : h * query_len + c * 16 + 16] = b
        return carry

    lax.fori_loop(0, pair_ref.shape[0], window, 0, unroll=3)


def block_kernel(
    atoms_ref,
    info_ref,
    cond_ref,
    left_ref,
    right_ref,
    bias_ref,
    lhs_ref,
    ada_w_ref,
    ada_b_ref,
    zero_w_ref,
    zero_b_ref,
    qkvg_ref,
    query_b_ref,
    out_w_ref,
    swiglu_ref,
    down_ref,
    token_w_ref,
    atoms_hbm,
    tokens_hbm,
    scale0,
    shift0,
    scale1,
    shift1,
    gate0,
    gate1,
    edge_bias,
    live_ref,
    onehot_ref,
    inverse_ref,
    q_ref,
    k_ref,
    v_ref,
    gate_ref,
    blend_ref,
    atoms_out_ref,
    tokens_out_ref,
    sems,
):
    samples, atom_dev, width = atoms_ref.shape
    windows, score_rows, key_len = bias_ref.shape
    query_len = atom_dev // windows
    heads = score_rows // query_len
    head_dim = width // heads
    margin = (key_len - query_len) // 2
    tok_dev = atom_dev // ATOMS_PER_TOKEN
    ext = atom_dev + 2 * HALO
    rows = atom_dev + 2 * EDGE
    first = HALO - EDGE
    hidden = down_ref.shape[0]

    at = 4 * HALO
    cond = jnp.concatenate(
        [left_ref[at : at + HALO], cond_ref[...], right_ref[at : at + HALO]], axis=0
    )
    norm = norm_rows(cond.astype(F32)).astype(BF16)
    adapt = dot(norm, ada_w_ref[0])
    scale0[...] = sigmoid(adapt[:, :width] + ada_b_ref[0:1])
    shift0[...] = adapt[:, width:]
    norm = norm[first : first + rows]
    adapt = dot(norm, ada_w_ref[1])
    scale1[...] = sigmoid(adapt[:, :width] + ada_b_ref[1:2])
    shift1[...] = adapt[:, width:]
    gate0[...] = sigmoid(dot(norm, zero_w_ref[0]) + zero_b_ref[0:1])
    gate1[...] = sigmoid(dot(norm, zero_w_ref[1]) + zero_b_ref[1:2])
    at += HALO
    for e, ref in enumerate((left_ref, right_ref)):
        x = ref[at : at + EDGE_Q * 16]
        x = jnp.concatenate([x, jnp.zeros_like(x)], axis=0)
        for h, b in enumerate(pair_bias(x, lhs_ref[...], 16, heads)):
            edge_bias[e, h * EDGE_Q : (h + 1) * EDGE_Q] = b[:EDGE_Q]
    at += EDGE_Q * 16
    usable = info_ref[0:1]
    own = info_ref[1:2]
    info_l = left_ref[at : at + 16].astype(F32)
    info_r = right_ref[at : at + 16].astype(F32)
    flags = jnp.concatenate([info_l[0:1], usable, info_r[0:1]], axis=1)
    tokens = jnp.concatenate(
        [info_l[1:2] - tok_dev, own, info_r[1:2] + tok_dev], axis=1
    )
    total = flags.shape[1]
    flags8 = jnp.broadcast_to(flags, (8, total))
    rolled = {}
    for w in range(-1, windows + 1):
        start = 128 + query_len * w - margin
        shift = start % 128
        if shift not in rolled:
            rolled[shift] = pltpu.roll(flags8, total - shift, 1)
        lane = start - shift
        row = rolled[shift][0:1, lane : lane + key_len]
        live_ref[w + 1 : w + 2] = jnp.where(row > 0.5, 0.0, MASKED)
    shift = 128 - EDGE
    flags = pltpu.roll(flags8, total - shift, 1)[0:1]
    tokens = pltpu.roll(jnp.broadcast_to(tokens, (8, total)), total - shift, 1)[0:1]
    lanes = onehot_ref.shape[1]
    slot = iota((tok_dev, lanes), 0).astype(F32)
    inside = iota((tok_dev, lanes), 1) < rows
    hit = (tokens[:, :lanes] == slot) & (flags[:, :lanes] > 0.5) & inside
    onehot = jnp.where(hit, 1.0, 0.0)
    onehot_ref[...] = onehot.astype(BF16)
    counts = jnp.sum(onehot, -1, keepdims=True)
    inverse_ref[...] = jnp.broadcast_to(1.0 / jnp.maximum(counts, 1.0), inverse_ref.shape)
    v_ref[:, width:] = jnp.ones((ext, width), BF16)

    lane_head = iota((1, width), 1) // head_dim

    def attend(q, keys_at, bias, live):
        n = q.shape[0]
        wide = jnp.concatenate(
            [jnp.where(lane_head == h, q, 0.0) for h in range(heads)], axis=0
        ).astype(BF16)
        scores = dot_t(wide, k_ref[keys_at : keys_at + key_len]) + (bias + live)
        top = jnp.max(scores, -1, keepdims=True)
        weights = jnp.exp(scores - top).astype(BF16)
        out = dot(weights, v_ref[keys_at : keys_at + key_len])
        pick = out[0:n]
        for h in range(1, heads):
            head = jnp.concatenate([lane_head, lane_head], axis=1)
            pick = jnp.where(head == h, out[h * n : (h + 1) * n], pick)
        return pick[:, :width] / pick[:, width:]

    def out_copies(sample):
        return (
            pltpu.make_async_copy(
                atoms_out_ref.at[sample], atoms_hbm.at[sample], sems.at[0, sample]
            ),
            pltpu.make_async_copy(
                tokens_out_ref.at[sample], tokens_hbm.at[sample], sems.at[1, sample]
            ),
        )

    def one_sample(sample, carry):
        at = pl.multiple_of(sample * HALO, 16)
        stream = jnp.concatenate(
            [left_ref[pl.ds(at, HALO)], atoms_ref[sample], right_ref[pl.ds(at, HALO)]], axis=0
        ).astype(F32)
        attn_in = (norm_rows(stream) * scale0[...] + shift0[...]).astype(BF16)
        keyval = dot(attn_in, qkvg_ref[:, width : 3 * width])
        k_ref[...] = keyval[:, :width].astype(BF16)
        v_ref[:, :width] = keyval[:, width:].astype(BF16)
        inner = attn_in[first : first + rows]
        factor = head_dim ** (-0.5)
        queries = dot(inner, qkvg_ref[:, :width])
        q_ref[...] = (queries + query_b_ref[0:1]) * factor
        gate_ref[...] = sigmoid(dot(inner, qkvg_ref[:, 3 * width :]))

        for w in range(windows):
            r = EDGE + w * query_len
            got = attend(
                q_ref[r : r + query_len],
                HALO + w * query_len - margin,
                bias_ref[w],
                live_ref[w + 1 : w + 2],
            )
            blend_ref[r : r + query_len] = (got * gate_ref[r : r + query_len]).astype(BF16)
        for e in range(2):
            r = (EDGE - EDGE_Q, EDGE + atom_dev)[e]
            w = (-1, windows)[e]
            got = attend(
                q_ref[r : r + EDGE_Q],
                HALO + w * query_len - margin,
                edge_bias[e],
                live_ref[w + 1 : w + 2],
            )
            got = got * gate_ref[r : r + EDGE_Q]
            pad = jnp.zeros_like(got)
            both = jnp.concatenate([pad, got] if e == 0 else [got, pad], axis=0)
            b = (0, EDGE + atom_dev)[e]
            blend_ref[b : b + EDGE] = both.astype(BF16)

        after = (
            stream[first : first + rows] + gate0[...] * dot(blend_ref[...], out_w_ref[...])
        ).astype(BF16)
        after32 = after.astype(F32)
        trans_in = (norm_rows(after32) * scale1[...] + shift1[...]).astype(BF16)
        mixed = dot(trans_in, swiglu_ref[...])
        a = mixed[:, :hidden]
        units = (a * sigmoid(a) * mixed[:, hidden:]).astype(BF16)
        result = (after32 + gate1[...] * dot(units, down_ref[...])).astype(BF16)
        atoms_out_ref[sample] = result[EDGE : EDGE + atom_dev]
        features = jnp.maximum(dot(result, token_w_ref[...]), 0.0).astype(BF16)
        totals = dot(onehot_ref[:, :rows], features)
        for c in range(0, totals.shape[1], 128):
            tokens_out_ref[sample, :, c : c + 128] = (totals[:, c : c + 128] * inverse_ref[...]).astype(
                BF16
            )
        for c in out_copies(sample):
            c.start()
        return carry

    lax.fori_loop(0, samples, one_sample, 0)
    for sample in range(samples):
        for c in out_copies(sample):
            c.wait()


def on_device(
    atoms_in,
    cond,
    pair,
    atom_mask,
    atom_count,
    atom_to_token,
    ada_weight,
    ada_bias,
    zero_weight,
    zero_bias,
    qkvg_weight,
    query_bias,
    pair_weight,
    out_weight,
    swiglu_weight,
    down_weight,
    token_weight,
):
    samples, atom_dev, width = atoms_in.shape
    windows, query_len, channels, key_len = pair.shape
    heads = pair_weight.shape[0]
    hidden = down_weight.shape[0]
    token_width = token_weight.shape[1]
    tok_dev = atom_dev // ATOMS_PER_TOKEN
    ext = atom_dev + 2 * HALO
    rows = atom_dev + 2 * EDGE
    smem = pl.BlockSpec(memory_space=pltpu.SMEM)
    far = pl.BlockSpec(memory_space=pltpu.HBM)
    vmem = pl.BlockSpec(memory_space=pltpu.VMEM)

    def near(array):
        return pltpu.with_memory_space_constraint(array, pltpu.VMEM)

    def away(array):
        return pltpu.with_memory_space_constraint(array, pltpu.HBM)

    wire_rows = (samples + 1) * HALO + EDGE_Q * channels + 16
    wire = pltpu.VMEM((wire_rows, width), BF16)
    pair = pair.reshape(windows, query_len * channels, key_len)
    up, down, info = pl.pallas_call(
        pack_kernel,
        out_shape=(wire, wire, pltpu.VMEM((16, atom_dev), F32)),
        in_specs=[smem] + [far] * 5,
        out_specs=(vmem, vmem, vmem),
        scratch_shapes=[
            pltpu.VMEM((atom_dev,), jnp.int32),
            pltpu.VMEM((atom_dev,), jnp.int32),
            pltpu.SemaphoreType.DMA((2 * (samples + 3),)),
        ],
        compiler_params=pltpu.CompilerParams(vmem_limit_bytes=4 << 20),
        name="pack",
    )(atom_count, *[away(a) for a in (atom_mask, atom_to_token, atoms_in, cond, pair)])
    count = lax.axis_size("atom")
    to_right = [(i, i + 1) for i in range(count - 1)]
    to_left = [(i + 1, i) for i in range(count - 1)]
    left = lax.ppermute(up, "atom", to_right)
    right = lax.ppermute(down, "atom", to_left)

    lhs_shape = (16 * channels + 3 * 16 * heads, 16 * channels)
    bias, lhs = pl.pallas_call(
        bias_kernel,
        out_shape=(
            pltpu.VMEM((windows, heads * query_len, key_len), F32),
            pltpu.VMEM(lhs_shape, BF16),
        ),
        in_specs=[vmem, vmem],
        out_specs=(vmem, vmem),
        compiler_params=pltpu.CompilerParams(vmem_limit_bytes=8 << 20),
        name="bias",
    )(pair_weight, near(pair))

    weights = (
        ada_weight,
        ada_bias,
        zero_weight,
        zero_bias,
        qkvg_weight,
        query_bias.reshape(1, width),
        out_weight,
        swiglu_weight,
        down_weight,
        token_weight,
    )
    operands = (atoms_in, info, cond, left, right, bias, lhs) + weights
    return pl.pallas_call(
        block_kernel,
        out_shape=(
            jax.ShapeDtypeStruct((samples, atom_dev, width), BF16),
            jax.ShapeDtypeStruct((samples, tok_dev, token_width), BF16),
        ),
        in_specs=[vmem] * len(operands),
        out_specs=(far, far),
        scratch_shapes=[
            pltpu.VMEM((ext, width), F32),
            pltpu.VMEM((ext, width), F32),
            pltpu.VMEM((rows, width), F32),
            pltpu.VMEM((rows, width), F32),
            pltpu.VMEM((rows, width), F32),
            pltpu.VMEM((rows, width), F32),
            pltpu.VMEM((2, heads * EDGE_Q, key_len), F32),
            pltpu.VMEM((16, key_len), F32),
            pltpu.VMEM((tok_dev, 512), BF16),
            pltpu.VMEM((tok_dev, 128), F32),
            pltpu.VMEM((rows, width), F32),
            pltpu.VMEM((ext, width), BF16),
            pltpu.VMEM((ext, 2 * width), BF16),
            pltpu.VMEM((rows, width), F32),
            pltpu.VMEM((rows, width), BF16),
            pltpu.VMEM((samples, atom_dev, width), BF16),
            pltpu.VMEM((samples, tok_dev, token_width), BF16),
            pltpu.SemaphoreType.DMA((2, samples)),
        ],
        compiler_params=pltpu.CompilerParams(vmem_limit_bytes=24 << 20),
        name="block",
    )(*[near(a) for a in operands])


def solution(mesh):
    in_specs = (
        P("struct", "atom", None),
        P(("struct", "atom"), None),
        P(("struct", "atom"), None, None, None),
        P(("struct", "atom")),
        P("struct"),
        P(("struct", "atom")),
        P(),
        P(),
        P(),
        P(),
        P(),
        P(),
        P(),
        P(),
        P(),
        P(),
        P(),
    )
    out_specs = (P("struct", "atom", None), P("struct", "atom", None))
    return jax.shard_map(
        on_device, mesh=mesh, in_specs=in_specs, out_specs=out_specs, check_vma=False
    )
```

time: 46.7 us -> 31.1 us (0.67)
  Pallas kernels: 34.2 us -> 21.5 us
  local copies, waits for them, and re-layouts: 3.22 us -> 0.06 us
    pallas_call x3, Pallas kernels: 34.2 us -> 21.5 us  [the longest x1 15 us: on_device(): pl.pallas_call(block_kernel, out_shape=(jax.ShapeDtypeStruct((samples, at...]
    reshape x2 -> x0, local copies, waits for them, and re-layouts: 2.53 us -> none  [the longest x1 1.28 us: on_device(): mask = atom_mask.reshape(1, atom_dev)]
    unnamed x4 -> x28, local copies, waits for them, and re-layouts: 0.69 us -> 0.06 us
  transfers between devices with their start and end apart: 2 -> 2, of which waited for: 0 -> 0; matrix products, arithmetic and copies ran while one was open for 0% -> 0% of each run, Pallas kernels for 16% -> 18%
where the time goes in v2:
time: 31.1 us; the launch traced here: 31 us
  Pallas kernels  21.5 us (69%)
  starting transfers between devices  7.67 us (25%)
  between operations  1.66 us (5%)
    pallas_call x1, Pallas kernels, on_device(): pl.pallas_call(block_kernel, out_shape=(jax.ShapeDtypeStruct((samples, at...  15 us
    ppermute x1, starting transfers between devices, on_device(): right = lax.ppermute(down, 'atom', to_left)  5.75 us
    pallas_call x1, Pallas kernels, on_device(): pl.pallas_call(bias_kernel, out_shape=(pltpu.VMEM((windows, heads * query...  5.5 us
    ppermute x1, starting transfers between devices, on_device(): left = lax.ppermute(up, 'atom', to_right)  1.92 us
    pallas_call x1, Pallas kernels, on_device(): pl.pallas_call(pack_kernel, out_shape=(wire, wire, pltpu.VMEM((16, atom_d...  1.04 us
  transfers between devices with their start and end apart: 2, of which 0 were waited for; matrix products, arithmetic and copies ran while one was open for 0% of the time, Pallas kernels for 18%

profile of v2, /device:TPU:98, one launch (start us, length us, event | category | flops | bytes accessed | tf_op | source)
XLA Modules:
  0.0 31.0 jit_solution(2108162542067308447)
XLA Ops:
  0.6 0.0 copy-start
  0.6 0.0 copy-start.10
  1.4 0.0 copy-start.1
  1.4 0.0 copy-start.2
  1.4 0.0 copy-start.3
  1.4 0.0 copy-start.4
  1.5 0.0 copy-start.5
  1.5 0.0 copy-start.6
  1.5 0.0 copy-start.7
  1.5 0.0 copy-start.8
  1.5 0.0 copy-start.9
  1.5 0.0 copy-start.11
  1.5 0.0 copy-start.12
  1.5 0.0 copy-start.13
  1.5 1.0 %pack.1 = (bf16[544,128]{1,0:T(8,128)(2,1)S(1)}, bf16[544,128]{1,0:T(8,128)(2,1)S(1)}, f32[16,384]{1,0:T(8,128)S(1)}) custom-call(s32[1]{0:T(128)S(6)} %copy.19.count_ref, s32[384]{0:T(512)} %mask_hbm.1, s32[384]{0:T(512)} %token_hbm.1, bf16[4,384,128]{2,1,0:T(8,128)(2,1)} %atoms_ref.3, bf16[384,128]{1,0:T(8,128)(2,1)} %cond_ref.3, bf16[12,512,128]{2,1,0:T(8,128)(2,1)} %bitcast.2), custom_call_target="tpu_custom_call" | custom-call | tf_op jit(solution)/shard_map/pack/pallas_call | solution.py:390
  2.6 1.9 %collective-permute-start = (bf16[544,128]{1,0:T(8,128)(2,1)S(1)}, bf16[544,128]{1,0:T(8,128)(2,1)S(1)}, u32[]{:S(2)}, u32[]{:S(2)}) collective-permute-start(bf16[544,128]{1,0:T(8,128)(2,1)S(1)} %get-tuple-element.8), channel_id=1, source_target_pairs={{0,1},{1,2},{2,3},{3,4},{4,5},{5,6},{6,7},{7,8},{8,9},{9,10},{10,1... | collective-permute-start | bytes 417800 | tf_op jit(solution)/shard_map/ppermute | solution.py:406
  4.5 5.8 %collective-permute-start.1 = (bf16[544,128]{1,0:T(8,128)(2,1)S(1)}, bf16[544,128]{1,0:T(8,128)(2,1)S(1)}, u32[]{:S(2)}, u32[]{:S(2)}) collective-permute-start(bf16[544,128]{1,0:T(8,128)(2,1)S(1)} %get-tuple-element.9), channel_id=1, source_target_pairs={{1,0},{2,1},{3,2},{4,3},{5,4},{6,5},{7,6},{8,7},{9,8},{10,9},{11,1... | collective-permute-start | bytes 417800 | tf_op jit(solution)/shard_map/ppermute | solution.py:407
  10.3 0.0 copy-done
  10.3 0.0 copy-done.10
  10.3 5.5 %bias.1 = (f32[12,128,128]{2,1,0:T(8,128)S(1)}, bf16[448,256]{1,0:T(8,128)(2,1)S(1)}) custom-call(f32[4,16]{1,0:T(4,128)S(1)} %copy-done.10, bf16[12,512,128]{2,1,0:T(8,128)(2,1)S(1)} %bitcast.3), custom_call_target="tpu_custom_call" | custom-call | tf_op jit(solution)/shard_map/bias/pallas_call | solution.py:410
  15.8 0.0 collective-permute-done.left_ref
  15.8 0.0 collective-permute-done.1.right_ref
  15.8 0.0 copy-done.1
  15.9 0.0 copy-done.2
  15.9 0.0 copy-done.3
  15.9 0.0 copy-done.4
  15.9 0.0 copy-done.5
  15.9 0.0 copy-done.6
  15.9 0.0 copy-done.7
  15.9 0.0 copy-done.8
  15.9 0.0 copy-done.9
  15.9 0.0 copy-done.11
  15.9 0.0 copy-done.12
  16.0 0.0 copy-done.13
  16.0 15.0 %block.1 = (bf16[4,384,128]{2,1,0:T(8,128)(2,1)}, bf16[4,48,768]{2,1,0:T(8,128)(2,1)}) custom-call(bf16[4,384,128]{2,1,0:T(8,128)(2,1)S(1)} %copy-done.1, f32[16,384]{1,0:T(8,128)S(1)} %get-tuple-element.7.info_ref, bf16[384,128]{1,0:T(8,128)(2,1)S(1)} %copy-done.2, bf16[544,128]{1,0:T(8,128)(2,1)S(1)} %collective-permute-done.left_ref, ...), custom_call_target="tpu_custom_call" | custom-call | tf_op jit(solution)/shard_map/block/pallas_call | solution.py:435
Async XLA Ops:
  0.6 9.6 %copy-start = (bf16[12,32,16,128]{3,2,1,0:T(8,128)(2,1)S(1)}, bf16[12,32,16,128]{3,2,1,0:T(8,128)(2,1)}, u32[]{:S(2)}) copy-start(bf16[12,32,16,128]{3,2,1,0:T(8,128)(2,1)} %param.19) | copy-start | bytes 4718596
  0.6 9.6 %copy-start.10 = (f32[4,16]{1,0:T(4,128)S(1)}, f32[4,16]{1,0:T(4,128)}, u32[]{:S(2)}) copy-start(f32[4,16]{1,0:T(4,128)} %weight_ref.1) | copy-start | bytes 772
  1.4 14.4 %copy-start.1 = (bf16[4,384,128]{2,1,0:T(8,128)(2,1)S(1)}, bf16[4,384,128]{2,1,0:T(8,128)(2,1)}, u32[]{:S(2)}) copy-start(bf16[4,384,128]{2,1,0:T(8,128)(2,1)} %atoms_ref.3) | copy-start | bytes 1179652
  1.4 14.4 %copy-start.2 = (bf16[384,128]{1,0:T(8,128)(2,1)S(1)}, bf16[384,128]{1,0:T(8,128)(2,1)}, u32[]{:S(2)}) copy-start(bf16[384,128]{1,0:T(8,128)(2,1)} %cond_ref.3) | copy-start | bytes 294916
  1.4 14.4 %copy-start.3 = (bf16[128,768]{1,0:T(8,128)(2,1)S(1)}, bf16[128,768]{1,0:T(8,128)(2,1)}, u32[]{:S(2)}) copy-start(bf16[128,768]{1,0:T(8,128)(2,1)} %token_w_ref.1) | copy-start | bytes 589828
  1.4 14.4 %copy-start.4 = (bf16[2,128,256]{2,1,0:T(8,128)(2,1)S(1)}, bf16[2,128,256]{2,1,0:T(8,128)(2,1)}, u32[]{:S(2)}) copy-start(bf16[2,128,256]{2,1,0:T(8,128)(2,1)} %ada_w_ref.1) | copy-start | bytes 393220
  1.5 14.4 %copy-start.5 = (bf16[128,512]{1,0:T(8,128)(2,1)S(1)}, bf16[128,512]{1,0:T(8,128)(2,1)}, u32[]{:S(2)}) copy-start(bf16[128,512]{1,0:T(8,128)(2,1)} %qkvg_ref.1) | copy-start | bytes 393220
  1.5 14.4 %copy-start.6 = (bf16[128,512]{1,0:T(8,128)(2,1)S(1)}, bf16[128,512]{1,0:T(8,128)(2,1)}, u32[]{:S(2)}) copy-start(bf16[128,512]{1,0:T(8,128)(2,1)} %swiglu_ref.1) | copy-start | bytes 393220
  1.5 14.4 %copy-start.7 = (bf16[2,128,128]{2,1,0:T(8,128)(2,1)S(1)}, bf16[2,128,128]{2,1,0:T(8,128)(2,1)}, u32[]{:S(2)}) copy-start(bf16[2,128,128]{2,1,0:T(8,128)(2,1)} %zero_w_ref.1) | copy-start | bytes 196612
  1.5 14.4 %copy-start.8 = (bf16[256,128]{1,0:T(8,128)(2,1)S(1)}, bf16[256,128]{1,0:T(8,128)(2,1)}, u32[]{:S(2)}) copy-start(bf16[256,128]{1,0:T(8,128)(2,1)} %down_ref.1) | copy-start | bytes 196612
  1.5 14.4 %copy-start.9 = (bf16[128,128]{1,0:T(8,128)(2,1)S(1)}, bf16[128,128]{1,0:T(8,128)(2,1)}, u32[]{:S(2)}) copy-start(bf16[128,128]{1,0:T(8,128)(2,1)} %out_w_ref.1) | copy-start | bytes 98308
  1.5 14.4 %copy-start.11 = (f32[2,128]{1,0:T(2,128)S(1)}, f32[2,128]{1,0:T(2,128)}, u32[]{:S(2)}) copy-start(f32[2,128]{1,0:T(2,128)} %ada_b_ref.1) | copy-start | bytes 3076
  1.5 14.4 %copy-start.12 = (f32[2,128]{1,0:T(2,128)S(1)}, f32[2,128]{1,0:T(2,128)}, u32[]{:S(2)}) copy-start(f32[2,128]{1,0:T(2,128)} %zero_b_ref.1) | copy-start | bytes 3076
  1.5 14.4 %copy-start.13 = (f32[128]{0:T(128)S(1)}, f32[128]{0:T(128)}, u32[]{:S(2)}) copy-start(f32[128]{0:T(128)} %param.28) | copy-start | bytes 1540
  2.6 13.2 %collective-permute-start = (bf16[544,128]{1,0:T(8,128)(2,1)S(1)}, bf16[544,128]{1,0:T(8,128)(2,1)S(1)}, u32[]{:S(2)}, u32[]{:S(2)}) collective-permute-start(bf16[544,128]{1,0:T(8,128)(2,1)S(1)} %get-tuple-element.8), channel_id=1, source_target_pairs={{0,1},{1,2},{2,3},{3,4},{4,5},{5,6},{6,7},{7,8},{8,9},{9,10},{10,1... | collective-permute-start | bytes 417800 | tf_op jit(solution)/shard_map/ppermute | solution.py:406
  4.5 11.3 %collective-permute-start.1 = (bf16[544,128]{1,0:T(8,128)(2,1)S(1)}, bf16[544,128]{1,0:T(8,128)(2,1)S(1)}, u32[]{:S(2)}, u32[]{:S(2)}) collective-permute-start(bf16[544,128]{1,0:T(8,128)(2,1)S(1)} %get-tuple-element.9), channel_id=1, source_target_pairs={{1,0},{2,1},{3,2},{4,3},{5,4},{6,5},{7,6},{8,7},{9,8},{10,9},{11,1... | collective-permute-start | bytes 417800 | tf_op jit(solution)/shard_map/ppermute | solution.py:407

commit v3 on v2

v3 whole, which is shorter than its diff:
```python
import functools

import jax
import jax.numpy as jnp
from jax import lax
from jax.experimental import pallas as pl
from jax.experimental.pallas import tpu as pltpu
from jax.sharding import PartitionSpec as P

ATOMS_PER_TOKEN = 8
EPS = 1e-05
HALO = 80
EDGE = 16
EDGE_Q = 8
MASKED = -1e30
BF16 = jnp.bfloat16
F32 = jnp.float32


def dot(a, b):
    return jnp.dot(a, b, preferred_element_type=F32)


def dot_t(a, b):
    return lax.dot_general(a, b, (((1,), (1,)), ((), ())), preferred_element_type=F32)


def norm_rows(x):
    center = jnp.mean(x, -1, keepdims=True)
    off = x - center
    spread = jnp.mean(jnp.square(off), -1, keepdims=True)
    return off * lax.rsqrt(spread + EPS)


def sigmoid(x):
    return 0.5 * jnp.tanh(0.5 * x) + 0.5


def iota(shape, dim):
    return lax.broadcasted_iota(jnp.int32, shape, dim)


def pack_kernel(
    count_ref,
    mask_hbm,
    token_hbm,
    atoms_ref,
    cond_ref,
    pair_ref,
    across_ref,
    within_ref,
    info_ref,
    mask_ref,
    token_ref,
    sems,
):
    samples, atom_dev, _ = atoms_ref.shape
    windows, pair_rows, _ = pair_ref.shape
    edge_rows = EDGE_Q * 16
    copies = []

    def copy(src, dst):
        c = pltpu.make_async_copy(src, dst, sems.at[len(copies)])
        c.start()
        copies.append(c)

    copy(mask_hbm, mask_ref)
    copy(token_hbm, token_ref)
    rows = (samples + 1) * HALO
    device = lax.axis_index("atom")
    odd = device % 2
    for wire, last in ((across_ref, odd), (within_ref, 1 - odd)):
        at = pl.multiple_of(last * (atom_dev - HALO), 16)
        w = last * (windows - 1)
        p = pl.multiple_of(last * (pair_rows - edge_rows), 16)
        for s in range(samples):
            copy(atoms_ref.at[s, pl.ds(at, HALO)], wire.at[pl.ds(s * HALO, HALO)])
        copy(cond_ref.at[pl.ds(at, HALO)], wire.at[pl.ds(samples * HALO, HALO)])
        copy(pair_ref.at[w, pl.ds(p, edge_rows)], wire.at[pl.ds(rows, edge_rows)])
    rows += edge_rows
    position = device * atom_dev + iota((1, atom_dev), 1)
    for c in copies[:2]:
        c.wait()
    mask = mask_ref[...].reshape(1, atom_dev)
    token = token_ref[...].reshape(1, atom_dev)
    usable = jnp.where((mask == 1) & (position < count_ref[0]), 1.0, 0.0)
    own = (token - device * (atom_dev // ATOMS_PER_TOKEN)).astype(F32)
    row = iota((16, atom_dev), 0)
    info = jnp.where(row == 0, usable, jnp.where(row == 1, own, 0.0))
    info_ref[...] = info
    end = info[:, atom_dev - 128 :]
    start = info[:, :128]
    across_ref[rows : rows + 16] = jnp.where(odd == 1, end, start).astype(BF16)
    within_ref[rows : rows + 16] = jnp.where(odd == 1, start, end).astype(BF16)
    for c in copies[2:]:
        c.wait()


def pair_lhs(weight_ref, lhs_ref):
    heads, channels = weight_ref.shape
    wide = 16 * channels
    w = weight_ref[...]
    w = w - jnp.mean(w, -1, keepdims=True)
    spread = jnp.where(iota((channels, wide), 1) % channels == iota((channels, wide), 0), 1.0, 0.0)
    tiled = jnp.dot(w, spread, precision=lax.Precision.HIGHEST, preferred_element_type=F32)
    full = jnp.concatenate(
        [jnp.broadcast_to(tiled[h : h + 1], (16, wide)) for h in range(heads)], axis=0
    )
    shape = (16 * heads, wide)
    full = jnp.where(iota(shape, 1) // channels == iota(shape, 0) % 16, full, 0.0)
    high = full.astype(BF16)
    rest = full - high.astype(F32)
    mid = rest.astype(BF16)
    low = (rest - mid.astype(F32)).astype(BF16)
    shape = (wide, wide)
    mean = jnp.where(iota(shape, 0) // channels == iota(shape, 1) // channels, 1.0 / channels, 0.0)
    n = 16 * heads
    lhs_ref[0:wide] = mean.astype(BF16)
    lhs_ref[wide : wide + n] = high
    lhs_ref[wide + n : wide + 2 * n] = mid
    lhs_ref[wide + 2 * n : wide + 3 * n] = low


def pair_sums(x, lhs, heads):
    n = 16 * heads
    out = dot(lhs, x)
    off = x.astype(F32) - out[0:256]
    square = off * off
    half = jnp.sum(square.reshape(16, 2, 8, -1), axis=1).reshape(128, -1)
    high = half.astype(BF16)
    low = (half - high.astype(F32)).astype(BF16)
    sums = out[256 : 256 + n] + out[256 + n : 256 + 2 * n] + out[256 + 2 * n : 256 + 3 * n]
    return sums, high, low


def pair_scale(sums, high, low):
    gather = jnp.where(iota((16, 128), 1) // 8 == iota((16, 128), 0), 1.0 / 16, 0.0).astype(BF16)
    rstd = lax.rsqrt(dot(gather, high) + dot(gather, low) + EPS)
    return sums * jnp.concatenate([rstd] * (sums.shape[0] // 16), axis=0)


def live_rows(flags, wanted, query_len, key_len, live_ref):
    total = flags.shape[1]
    flags8 = jnp.broadcast_to(flags, (8, total))
    rolled = {}
    for n, w in wanted:
        start = 128 + query_len * w - (key_len - query_len) // 2
        shift = start % 128
        if shift not in rolled:
            rolled[shift] = pltpu.roll(flags8, total - shift, 1)
        row = rolled[shift][0:1, start - shift : start - shift + key_len]
        live_ref[n : n + 1] = jnp.where(row > 0.5, 0.0, MASKED)


def bias_kernel(weight_ref, info_ref, pair_ref, bias_ref, lhs_ref, sum_ref, half_ref, live_ref):
    heads = weight_ref.shape[0]
    windows, score_rows, key_len = bias_ref.shape
    query_len = score_rows // heads
    pair_lhs(weight_ref, lhs_ref)
    ones = jnp.ones((1, 128), F32)
    flags = jnp.concatenate([ones, info_ref[0:1], ones], axis=1)
    live_rows(flags, [(w, w) for w in range(windows)], query_len, key_len, live_ref)
    per = query_len // 16
    n = 16 * heads

    def first(c):
        x = pair_ref[c // per, c % per * 256 : c % per * 256 + 256]
        sum_ref[c % 4], half_ref[c % 4, 0], half_ref[c % 4, 1] = pair_sums(
            x, lhs_ref[...], heads
        )

    def second(c):
        got = pair_scale(sum_ref[c % 4], half_ref[c % 4, 0], half_ref[c % 4, 1])
        w = c // per
        live = live_ref[w : w + 1]
        for h in range(heads):
            at = h * query_len + c % per * 16
            bias_ref[w, at : at + 16] = got[h * 16 : h * 16 + 16] + live

    chunks = range(windows * per)
    weave(
        skew([lambda c=c: first(c) for c in chunks], [lambda c=c: second(c) for c in chunks])
    )


PIECES = 4


def weave(*streams):
    steps = [x for x in streams if x]
    total = max(len(x) for x in steps)
    done = [0] * len(steps)
    for t in range(total):
        for n, x in enumerate(steps):
            while done[n] * total < (t + 1) * len(x) and done[n] < len(x):
                x[done[n]]()
                done[n] += 1


def skew(*stages):
    pieces = len(stages[0])
    out = []
    for t in range(pieces + len(stages) - 1):
        for n, stage in enumerate(stages):
            if 0 <= t - n < pieces:
                out.append(stage[t - n])
    return out


def block_kernel(
    atoms_ref,
    info_ref,
    cond_ref,
    across_ref,
    within_ref,
    bias_ref,
    lhs_ref,
    ada_w_ref,
    ada_b_ref,
    zero_w_ref,
    zero_b_ref,
    qkvg_ref,
    query_b_ref,
    out_w_ref,
    swiglu_ref,
    down_ref,
    token_w_ref,
    atoms_hbm,
    tokens_hbm,
    scale0,
    shift0,
    scale1,
    shift1,
    gate0,
    gate1,
    edge_bias,
    live_ref,
    onehot_ref,
    inverse_ref,
    left_ref,
    right_ref,
    norm_ref,
    wqg_ref,
    attn_ref,
    q_ref,
    k_ref,
    v_ref,
    gate_ref,
    score_ref,
    prob_ref,
    blend_ref,
    after_ref,
    trans_ref,
    hidden_ref,
    result_ref,
    feature_ref,
    tokens_ref,
    sems,
):
    samples, atom_dev, width = atoms_ref.shape
    windows, score_rows, key_len = bias_ref.shape
    query_len = atom_dev // windows
    heads = score_rows // query_len
    head_dim = width // heads
    margin = (key_len - query_len) // 2
    tok_dev = atom_dev // ATOMS_PER_TOKEN
    ext = atom_dev + 2 * HALO
    rows = atom_dev + 2 * EDGE
    first = HALO - EDGE
    hidden = down_ref.shape[0]
    token_width = token_w_ref.shape[1]
    factor = head_dim ** (-0.5)

    odd = lax.axis_index("atom") % 2 == 1
    left_ref[...] = jnp.where(odd, within_ref[...], across_ref[...])
    right_ref[...] = jnp.where(odd, across_ref[...], within_ref[...])
    at = samples * HALO
    wqg_ref[:, :width] = qkvg_ref[:, :width]
    wqg_ref[:, width:] = qkvg_ref[:, 3 * width :]
    at += HALO + EDGE_Q * 16
    usable = info_ref[0:1]
    own = info_ref[1:2]
    info_l = left_ref[at : at + 16].astype(F32)
    info_r = right_ref[at : at + 16].astype(F32)
    flags = jnp.concatenate([info_l[0:1], usable, info_r[0:1]], axis=1)
    tokens = jnp.concatenate([info_l[1:2] - tok_dev, own, info_r[1:2] + tok_dev], axis=1)
    total = flags.shape[1]
    halo = jnp.concatenate([info_l[0:1], jnp.ones_like(usable), info_r[0:1]], axis=1)
    inner = [(w + 1, w) for w in (0, 1, windows - 2, windows - 1)]
    live_rows(halo, inner, query_len, key_len, live_ref)
    outer = [(w + 1, w) for w in (-1, windows)]
    live_rows(flags, outer, query_len, key_len, live_ref)
    flags8 = jnp.broadcast_to(flags, (8, total))
    shift = 128 - EDGE
    flags = pltpu.roll(flags8, total - shift, 1)[0:1]
    tokens = pltpu.roll(jnp.broadcast_to(tokens, (8, total)), total - shift, 1)[0:1]
    lanes = onehot_ref.shape[1]
    slot = iota((tok_dev, lanes), 0).astype(F32)
    inside = iota((tok_dev, lanes), 1) < rows
    hit = (tokens[:, :lanes] == slot) & (flags[:, :lanes] > 0.5) & inside
    onehot = jnp.where(hit, 1.0, 0.0)
    onehot_ref[...] = onehot.astype(BF16)
    counts = jnp.sum(onehot, -1, keepdims=True)
    inverse_ref[...] = jnp.broadcast_to(1.0 / jnp.maximum(counts, 1.0), inverse_ref.shape)
    v_ref[:, :, width:] = jnp.ones((samples, ext, width), BF16)

    lane_head = iota((1, width), 1) // head_dim
    masks = [jnp.where(lane_head == h, 1.0, 0.0).astype(BF16) for h in range(heads)]
    pick_head = jnp.concatenate([lane_head, lane_head], axis=1)
    places = [
        (EDGE + w * query_len, query_len, HALO + w * query_len - margin, w)
        for w in range(windows)
    ]
    for w, r in ((-1, EDGE - EDGE_Q), (windows, EDGE + atom_dev)):
        places.append((r, EDGE_Q, HALO + w * query_len - margin, w))

    def spliced(middle, off, lo, hi):
        parts = []
        for base, size, ref, start in (
            (0, HALO, left_ref, off),
            (HALO, atom_dev, middle, 0),
            (HALO + atom_dev, HALO, right_ref, off),
        ):
            x, y = max(lo, base), min(hi, base + size)
            if x < y:
                parts.append(ref[x - base + start : y - base + start])
        return parts[0] if len(parts) == 1 else jnp.concatenate(parts, axis=0)

    def stream_rows(s, lo, hi):
        return spliced(atoms_ref.at[s], s * HALO, lo, hi)

    def each(step, n, pieces):
        size = -(-n // pieces // 16) * 16
        return [
            lambda lo=lo, hi=min(n, lo + size): step(lo, hi) for lo in range(0, n, size)
        ]

    def cond_piece(lo, hi):
        x = spliced(cond_ref, samples * HALO, lo, hi).astype(F32)
        norm = norm_rows(x).astype(BF16)
        norm_ref[lo:hi] = norm
        adapt = dot(norm, ada_w_ref[0])
        scale0[lo:hi] = sigmoid(adapt[:, :width] + ada_b_ref[0:1])
        shift0[lo:hi] = adapt[:, width:]

    def gates():
        def adapt_piece(lo, hi):
            adapt = dot(norm_ref[first + lo : first + hi], ada_w_ref[1])
            scale1[lo:hi] = sigmoid(adapt[:, :width] + ada_b_ref[1:2])
            shift1[lo:hi] = adapt[:, width:]

        def zero_piece(lo, hi):
            norm = norm_ref[first + lo : first + hi]
            gate0[lo:hi] = sigmoid(dot(norm, zero_w_ref[0]) + zero_b_ref[0:1])
            gate1[lo:hi] = sigmoid(dot(norm, zero_w_ref[1]) + zero_b_ref[1:2])

        def edge_piece(e):
            x = (left_ref, right_ref)[e]
            start = (samples + 1) * HALO
            x = x[start : start + EDGE_Q * 16]
            x = jnp.concatenate([x, jnp.zeros_like(x)], axis=0)
            got = pair_scale(*pair_sums(x, lhs_ref[...], heads))
            for h in range(heads):
                edge_bias[e, h * EDGE_Q : (h + 1) * EDGE_Q] = got[h * 16 : h * 16 + EDGE_Q]

        out = [lambda e=e: edge_piece(e) for e in range(2)]
        return out + skew(each(adapt_piece, rows, 4), each(zero_piece, rows, 4))

    def prepare(s):
        def norm_piece(lo, hi):
            x = stream_rows(s, lo, hi).astype(F32)
            y = norm_rows(x) * scale0[lo:hi] + shift0[lo:hi]
            attn_ref[s, lo:hi] = y.astype(BF16)

        def keyval_piece(lo, hi):
            y = dot(attn_ref[s, lo:hi], qkvg_ref[:, width : 3 * width])
            k_ref[s, lo:hi] = y[:, :width].astype(BF16)
            v_ref[s, lo:hi, :width] = y[:, width:].astype(BF16)

        def query_piece(lo, hi):
            lo, hi = max(lo - first, 0), min(hi - first, rows)
            y = dot(attn_ref[s, first + lo : first + hi], wqg_ref[...])
            q_ref[s, lo:hi] = ((y[:, :width] + query_b_ref[0:1]) * factor).astype(BF16)
            gate_ref[s, lo:hi] = sigmoid(y[:, width:])

        stages = [each(f, ext, 4) for f in (norm_piece, keyval_piece, query_piece)]
        if s == 0:
            stages = [each(cond_piece, ext, 4)] + stages
        return skew(*stages)

    def attend(s):
        def score(t):
            r, n, key, w = places[t]
            if n >= 16:
                q = q_ref[s, r : r + n]
                wide = jnp.concatenate([q * masks[h] for h in range(heads)], axis=0)
                bias = bias_ref[w]
            else:
                base = r // 16 * 16
                q = q_ref[s, base : base + 16].astype(F32)[r - base : r - base + n]
                wide = jnp.concatenate(
                    [jnp.where(lane_head == h, q, 0.0) for h in range(heads)], axis=0
                ).astype(BF16)
                bias = edge_bias[0 if w < 0 else 1]
            got = dot_t(wide, k_ref[s, key : key + key_len])
            if 1 < w < windows - 2:
                got = got + bias
            else:
                got = got + (bias + live_ref[w + 1 : w + 2])
            score_ref[s % 2, t, : heads * n] = got

        def soften(t):
            n = heads * places[t][1]
            x = score_ref[s % 2, t, :n]
            top = jnp.max(x, -1, keepdims=True)
            prob_ref[s % 2, t, :n] = jnp.exp(x - top).astype(BF16)

        def blend(t):
            r, n, key, w = places[t]
            out = dot(prob_ref[s % 2, t, : heads * n], v_ref[s, key : key + key_len])
            pick = out[0:n]
            for h in range(1, heads):
                pick = jnp.where(pick_head == h, out[h * n : (h + 1) * n], pick)
            got = pick[:, :width] / pick[:, width:] * gate_ref[s, r : r + n]
            if n < 16:
                pad = jnp.zeros_like(got)
                base = r // 16 * 16
                got = jnp.concatenate([pad, got] if r > base else [got, pad], axis=0)
                r, n = base, 16
            blend_ref[s, r : r + n] = got.astype(BF16)

        count = len(places)
        out = []
        for t in range(count + 2):
            if t < count:
                out.append(lambda t=t: score(t))
            if 0 <= t - 1 < count:
                out.append(lambda t=t: soften(t - 1))
            if 0 <= t - 2 < count:
                out.append(lambda t=t: blend(t - 2))
        return out

    def out_copies(s):
        return (
            pltpu.make_async_copy(
                result_ref.at[s, pl.ds(EDGE, atom_dev)], atoms_hbm.at[s], sems.at[0, s]
            ),
            pltpu.make_async_copy(tokens_ref.at[s], tokens_hbm.at[s], sems.at[1, s]),
        )

    def finish(s):
        def after_piece(lo, hi):
            x = stream_rows(s, first + lo, first + hi).astype(F32)
            y = (x + gate0[lo:hi] * dot(blend_ref[s, lo:hi], out_w_ref[...])).astype(BF16)
            after_ref[s, lo:hi] = y
            z = norm_rows(y.astype(F32)) * scale1[lo:hi] + shift1[lo:hi]
            trans_ref[s, lo:hi] = z.astype(BF16)

        def hidden_piece(lo, hi):
            y = dot(trans_ref[s, lo:hi], swiglu_ref[...])
            a = y[:, :hidden]
            hidden_ref[s, lo:hi] = (a * sigmoid(a) * y[:, hidden:]).astype(BF16)

        def result_piece(lo, hi):
            y = gate1[lo:hi] * dot(hidden_ref[s, lo:hi], down_ref[...])
            result_ref[s, lo:hi] = (after_ref[s, lo:hi].astype(F32) + y).astype(BF16)

        def feature_piece(lo, hi):
            y = dot(result_ref[s, lo:hi], token_w_ref[...])
            feature_ref[s % 2, lo:hi] = jnp.maximum(y, 0.0).astype(BF16)

        def token_piece(lo, hi):
            y = dot(onehot_ref[:, :rows], feature_ref[s % 2, :, lo:hi])
            for c in range(lo, hi, 128):
                z = y[:, c - lo : c - lo + 128] * inverse_ref[...]
                tokens_ref[s, :, c : c + 128] = z.astype(BF16)

        def send():
            for c in out_copies(s):
                c.start()

        stages = (after_piece, hidden_piece, result_piece, feature_piece)
        out = skew(*[each(f, rows, PIECES) for f in stages])
        out += [lambda lo=lo: token_piece(lo, lo + 256) for lo in range(0, token_width, 256)]
        return out + [send]

    weave(prepare(0))
    for s in range(samples):
        weave(
            attend(s),
            finish(s - 1) if s > 0 else gates(),
            prepare(s + 1) if s + 1 < samples else None,
        )
    weave(finish(samples - 1))
    for s in range(samples):
        for c in out_copies(s):
            c.wait()


def on_device(
    atoms_in,
    cond,
    pair,
    atom_mask,
    atom_count,
    atom_to_token,
    ada_weight,
    ada_bias,
    zero_weight,
    zero_bias,
    qkvg_weight,
    query_bias,
    pair_weight,
    out_weight,
    swiglu_weight,
    down_weight,
    token_weight,
):
    samples, atom_dev, width = atoms_in.shape
    windows, query_len, channels, key_len = pair.shape
    heads = pair_weight.shape[0]
    hidden = down_weight.shape[0]
    token_width = token_weight.shape[1]
    tok_dev = atom_dev // ATOMS_PER_TOKEN
    ext = atom_dev + 2 * HALO
    rows = atom_dev + 2 * EDGE
    smem = pl.BlockSpec(memory_space=pltpu.SMEM)
    far = pl.BlockSpec(memory_space=pltpu.HBM)
    vmem = pl.BlockSpec(memory_space=pltpu.VMEM)

    def near(array):
        return pltpu.with_memory_space_constraint(array, pltpu.VMEM)

    def away(array):
        return pltpu.with_memory_space_constraint(array, pltpu.HBM)

    wire_rows = (samples + 1) * HALO + EDGE_Q * channels + 16
    wire = pltpu.VMEM((wire_rows, width), BF16)
    pair = pair.reshape(windows, query_len * channels, key_len)
    across, within, info = pl.pallas_call(
        pack_kernel,
        out_shape=(wire, wire, pltpu.VMEM((16, atom_dev), F32)),
        in_specs=[smem] + [far] * 5,
        out_specs=(vmem, vmem, vmem),
        scratch_shapes=[
            pltpu.VMEM((atom_dev,), jnp.int32),
            pltpu.VMEM((atom_dev,), jnp.int32),
            pltpu.SemaphoreType.DMA((2 * (samples + 3),)),
        ],
        compiler_params=pltpu.CompilerParams(vmem_limit_bytes=4 << 20),
        name="pack",
    )(atom_count, *[away(a) for a in (atom_mask, atom_to_token, atoms_in, cond, pair)])
    count = lax.axis_size("atom")
    swaps = [[(i, i + 1) for i in range(at, count - 1, 2)] for at in (1, 0)]
    swaps = [pairs + [(j, i) for i, j in pairs] for pairs in swaps]
    across = lax.ppermute(across, "atom", swaps[0])
    within = lax.ppermute(within, "atom", swaps[1])

    lhs_shape = (16 * channels + 3 * 16 * heads, 16 * channels)
    bias, lhs = pl.pallas_call(
        bias_kernel,
        out_shape=(
            pltpu.VMEM((windows, heads * query_len, key_len), F32),
            pltpu.VMEM(lhs_shape, BF16),
        ),
        in_specs=[vmem] * 3,
        out_specs=(vmem, vmem),
        scratch_shapes=[
            pltpu.VMEM((4, 16 * heads, key_len), F32),
            pltpu.VMEM((4, 2, 128, key_len), BF16),
            pltpu.VMEM((16, key_len), F32),
        ],
        compiler_params=pltpu.CompilerParams(vmem_limit_bytes=8 << 20),
        name="bias",
    )(pair_weight, near(info), near(pair))

    weights = (
        ada_weight,
        ada_bias,
        zero_weight,
        zero_bias,
        qkvg_weight,
        query_bias.reshape(1, width),
        out_weight,
        swiglu_weight,
        down_weight,
        token_weight,
    )
    operands = (atoms_in, info, cond, across, within, bias, lhs) + weights
    return pl.pallas_call(
        block_kernel,
        out_shape=(
            jax.ShapeDtypeStruct((samples, atom_dev, width), BF16),
            jax.ShapeDtypeStruct((samples, tok_dev, token_width), BF16),
        ),
        in_specs=[vmem] * len(operands),
        out_specs=(far, far),
        scratch_shapes=[
            pltpu.VMEM((ext, width), F32),
            pltpu.VMEM((ext, width), F32),
            pltpu.VMEM((rows, width), F32),
            pltpu.VMEM((rows, width), F32),
            pltpu.VMEM((rows, width), F32),
            pltpu.VMEM((rows, width), F32),
            pltpu.VMEM((2, heads * EDGE_Q, key_len), F32),
            pltpu.VMEM((16, key_len), F32),
            pltpu.VMEM((tok_dev, 512), BF16),
            pltpu.VMEM((tok_dev, 128), F32),
            pltpu.VMEM((wire_rows, width), BF16),
            pltpu.VMEM((wire_rows, width), BF16),
            pltpu.VMEM((ext, width), BF16),
            pltpu.VMEM((width, 2 * width), BF16),
            pltpu.VMEM((samples, ext, width), BF16),
            pltpu.VMEM((samples, rows, width), BF16),
            pltpu.VMEM((samples, ext, width), BF16),
            pltpu.VMEM((samples, ext, 2 * width), BF16),
            pltpu.VMEM((samples, rows, width), F32),
            pltpu.VMEM((2, windows + 2, heads * query_len, key_len), F32),
            pltpu.VMEM((2, windows + 2, heads * query_len, key_len), BF16),
            pltpu.VMEM((samples, rows, width), BF16),
            pltpu.VMEM((samples, rows, width), BF16),
            pltpu.VMEM((samples, rows, width), BF16),
            pltpu.VMEM((samples, rows, hidden), BF16),
            pltpu.VMEM((samples, rows, width), BF16),
            pltpu.VMEM((2, rows, token_width), BF16),
            pltpu.VMEM((samples, tok_dev, token_width), BF16),
            pltpu.SemaphoreType.DMA((2, samples)),
        ],
        compiler_params=pltpu.CompilerParams(vmem_limit_bytes=24 << 20),
        name="block",
    )(*[near(a) for a in operands])


def solution(mesh):
    in_specs = (
        P("struct", "atom", None),
        P(("struct", "atom"), None),
        P(("struct", "atom"), None, None, None),
        P(("struct", "atom")),
        P("struct"),
        P(("struct", "atom")),
        P(),
        P(),
        P(),
        P(),
        P(),
        P(),
        P(),
        P(),
        P(),
        P(),
        P(),
    )
    out_specs = (P("struct", "atom", None), P("struct", "atom", None))
    return jax.shard_map(
        on_device, mesh=mesh, in_specs=in_specs, out_specs=out_specs, check_vma=False
    )
```

time: 31.1 us -> 21.4 us (0.69)
  the two profiles are of different devices: /device:TPU:98 before, /device:TPU:7 now
where the time goes in v3:
time: 21.4 us; the launch traced here: 21.3 us
  Pallas kernels  14.2 us (66%)
  starting transfers between devices  5.39 us (25%)
  between operations  1.65 us (8%)
    pallas_call x1, Pallas kernels, on_device(): pl.pallas_call(block_kernel, out_shape=(jax.ShapeDtypeStruct((samples, at...  9.7 us
    ppermute x1, starting transfers between devices, on_device(): across = lax.ppermute(across, 'atom', swaps[0])  3.77 us
    pallas_call x1, Pallas kernels, on_device(): pl.pallas_call(bias_kernel, out_shape=(pltpu.VMEM((windows, heads * query...  3.44 us
    ppermute x1, starting transfers between devices, on_device(): within = lax.ppermute(within, 'atom', swaps[1])  1.62 us
    pallas_call x1, Pallas kernels, on_device(): pl.pallas_call(pack_kernel, out_shape=(wire, wire, pltpu.VMEM((16, atom_d...  1.04 us
  transfers between devices with their start and end apart: 2, of which 0 were waited for; matrix products, arithmetic and copies ran while one was open for 0% of the time, Pallas kernels for 16%

profile of v3, /device:TPU:7, one launch (start us, length us, event | category | flops | bytes accessed | tf_op | source)
XLA Modules:
  0.0 21.3 jit_solution(6012984439913854101)
XLA Ops:
  0.6 0.0 copy-start
  0.6 0.0 copy-start.10
  1.4 0.0 copy-start.1
  1.4 0.0 copy-start.2
  1.4 0.0 copy-start.3
  1.4 0.0 copy-start.4
  1.5 0.0 copy-start.5
  1.5 0.0 copy-start.6
  1.5 0.0 copy-start.7
  1.5 0.0 copy-start.8
  1.5 0.0 copy-start.9
  1.5 0.0 copy-start.11
  1.5 0.0 copy-start.12
  1.5 0.0 copy-start.13
  1.5 1.0 %pack.1 = (bf16[544,128]{1,0:T(8,128)(2,1)S(1)}, bf16[544,128]{1,0:T(8,128)(2,1)S(1)}, f32[16,384]{1,0:T(8,128)S(1)}) custom-call(s32[1]{0:T(128)S(6)} %copy.19.count_ref, s32[384]{0:T(512)} %mask_hbm.1, s32[384]{0:T(512)} %token_hbm.1, bf16[4,384,128]{2,1,0:T(8,128)(2,1)} %atoms_ref.3, bf16[384,128]{1,0:T(8,128)(2,1)} %cond_ref.3, bf16[12,512,128]{2,1,0:T(8,128)(2,1)} %bitcast.2), custom_call_target="tpu_custom_call" | custom-call | tf_op jit(solution)/shard_map/pack/pallas_call | solution.py:540
  2.6 3.8 %collective-permute-start = (bf16[544,128]{1,0:T(8,128)(2,1)S(1)}, bf16[544,128]{1,0:T(8,128)(2,1)S(1)}, u32[]{:S(2)}, u32[]{:S(2)}) collective-permute-start(bf16[544,128]{1,0:T(8,128)(2,1)S(1)} %get-tuple-element.8), channel_id=1, source_target_pairs={{1,2},{3,4},{5,6},{7,8},{9,10},{11,12},{13,14},{2,1},{4,3},{6,5},{... | collective-permute-start | bytes 417800 | tf_op jit(solution)/shard_map/ppermute | solution.py:556
  6.4 1.6 %collective-permute-start.1 = (bf16[544,128]{1,0:T(8,128)(2,1)S(1)}, bf16[544,128]{1,0:T(8,128)(2,1)S(1)}, u32[]{:S(2)}, u32[]{:S(2)}) collective-permute-start(bf16[544,128]{1,0:T(8,128)(2,1)S(1)} %get-tuple-element.9), channel_id=1, source_target_pairs={{0,1},{2,3},{4,5},{6,7},{8,9},{10,11},{12,13},{14,15},{1,0},{3,2},... | collective-permute-start | bytes 417800 | tf_op jit(solution)/shard_map/ppermute | solution.py:557
  8.0 0.0 copy-done
  8.0 0.0 copy-done.10
  8.0 3.4 %bias.1 = (f32[12,128,128]{2,1,0:T(8,128)S(1)}, bf16[448,256]{1,0:T(8,128)(2,1)S(1)}) custom-call(f32[4,16]{1,0:T(4,128)S(1)} %copy-done.10, f32[16,384]{1,0:T(8,128)S(1)} %get-tuple-element.7.info_ref, bf16[12,512,128]{2,1,0:T(8,128)(2,1)S(1)} %bitcast.3), custom_call_target="tpu_custom_call" | custom-call | tf_op jit(solution)/shard_map/bias/pallas_call | solution.py:560
  11.4 0.0 collective-permute-done.across_ref
  11.5 0.0 collective-permute-done.1.within_ref
  11.5 0.0 copy-done.1
  11.5 0.0 copy-done.2
  11.5 0.0 copy-done.3
  11.5 0.0 copy-done.4
  11.5 0.0 copy-done.5
  11.5 0.0 copy-done.6
  11.5 0.0 copy-done.7
  11.5 0.0 copy-done.8
  11.5 0.0 copy-done.9
  11.6 0.0 copy-done.11
  11.6 0.0 copy-done.12
  11.6 0.0 copy-done.13
  11.6 9.7 %block.1 = (bf16[4,384,128]{2,1,0:T(8,128)(2,1)}, bf16[4,48,768]{2,1,0:T(8,128)(2,1)}) custom-call(bf16[4,384,128]{2,1,0:T(8,128)(2,1)S(1)} %copy-done.1, f32[16,384]{1,0:T(8,128)S(1)} %get-tuple-element.7.info_ref, bf16[384,128]{1,0:T(8,128)(2,1)S(1)} %copy-done.2, bf16[544,128]{1,0:T(8,128)(2,1)S(1)} %collective-permute-done.across_ref, ...), custom_call_target="tpu_custom_call" | custom-call | tf_op jit(solution)/shard_map/block/pallas_call | solution.py:590
Async XLA Ops:
  0.6 7.4 %copy-start = (bf16[12,32,16,128]{3,2,1,0:T(8,128)(2,1)S(1)}, bf16[12,32,16,128]{3,2,1,0:T(8,128)(2,1)}, u32[]{:S(2)}) copy-start(bf16[12,32,16,128]{3,2,1,0:T(8,128)(2,1)} %param.19) | copy-start | bytes 4718596
  0.6 7.3 %copy-start.10 = (f32[4,16]{1,0:T(4,128)S(1)}, f32[4,16]{1,0:T(4,128)}, u32[]{:S(2)}) copy-start(f32[4,16]{1,0:T(4,128)} %weight_ref.1) | copy-start | bytes 772
  1.4 10.0 %copy-start.1 = (bf16[4,384,128]{2,1,0:T(8,128)(2,1)S(1)}, bf16[4,384,128]{2,1,0:T(8,128)(2,1)}, u32[]{:S(2)}) copy-start(bf16[4,384,128]{2,1,0:T(8,128)(2,1)} %atoms_ref.3) | copy-start | bytes 1179652
  1.4 10.0 %copy-start.2 = (bf16[384,128]{1,0:T(8,128)(2,1)S(1)}, bf16[384,128]{1,0:T(8,128)(2,1)}, u32[]{:S(2)}) copy-start(bf16[384,128]{1,0:T(8,128)(2,1)} %cond_ref.3) | copy-start | bytes 294916
  1.4 10.0 %copy-start.3 = (bf16[128,768]{1,0:T(8,128)(2,1)S(1)}, bf16[128,768]{1,0:T(8,128)(2,1)}, u32[]{:S(2)}) copy-start(bf16[128,768]{1,0:T(8,128)(2,1)} %token_w_ref.1) | copy-start | bytes 589828
  1.4 10.0 %copy-start.4 = (bf16[2,128,256]{2,1,0:T(8,128)(2,1)S(1)}, bf16[2,128,256]{2,1,0:T(8,128)(2,1)}, u32[]{:S(2)}) copy-start(bf16[2,128,256]{2,1,0:T(8,128)(2,1)} %ada_w_ref.1) | copy-start | bytes 393220
  1.5 10.0 %copy-start.5 = (bf16[128,512]{1,0:T(8,128)(2,1)S(1)}, bf16[128,512]{1,0:T(8,128)(2,1)}, u32[]{:S(2)}) copy-start(bf16[128,512]{1,0:T(8,128)(2,1)} %qkvg_ref.1) | copy-start | bytes 393220
  1.5 10.0 %copy-start.6 = (bf16[128,512]{1,0:T(8,128)(2,1)S(1)}, bf16[128,512]{1,0:T(8,128)(2,1)}, u32[]{:S(2)}) copy-start(bf16[128,512]{1,0:T(8,128)(2,1)} %swiglu_ref.1) | copy-start | bytes 393220
  1.5 10.0 %copy-start.7 = (bf16[2,128,128]{2,1,0:T(8,128)(2,1)S(1)}, bf16[2,128,128]{2,1,0:T(8,128)(2,1)}, u32[]{:S(2)}) copy-start(bf16[2,128,128]{2,1,0:T(8,128)(2,1)} %zero_w_ref.1) | copy-start | bytes 196612
  1.5 10.0 %copy-start.8 = (bf16[256,128]{1,0:T(8,128)(2,1)S(1)}, bf16[256,128]{1,0:T(8,128)(2,1)}, u32[]{:S(2)}) copy-start(bf16[256,128]{1,0:T(8,128)(2,1)} %down_ref.1) | copy-start | bytes 196612
  1.5 10.0 %copy-start.9 = (bf16[128,128]{1,0:T(8,128)(2,1)S(1)}, bf16[128,128]{1,0:T(8,128)(2,1)}, u32[]{:S(2)}) copy-start(bf16[128,128]{1,0:T(8,128)(2,1)} %out_w_ref.1) | copy-start | bytes 98308
  1.5 10.0 %copy-start.11 = (f32[2,128]{1,0:T(2,128)S(1)}, f32[2,128]{1,0:T(2,128)}, u32[]{:S(2)}) copy-start(f32[2,128]{1,0:T(2,128)} %ada_b_ref.1) | copy-start | bytes 3076
  1.5 10.0 %copy-start.12 = (f32[2,128]{1,0:T(2,128)S(1)}, f32[2,128]{1,0:T(2,128)}, u32[]{:S(2)}) copy-start(f32[2,128]{1,0:T(2,128)} %zero_b_ref.1) | copy-start | bytes 3076
  1.5 10.0 %copy-start.13 = (f32[128]{0:T(128)S(1)}, f32[128]{0:T(128)}, u32[]{:S(2)}) copy-start(f32[128]{0:T(128)} %param.28) | copy-start | bytes 1540
  2.6 8.9 %collective-permute-start = (bf16[544,128]{1,0:T(8,128)(2,1)S(1)}, bf16[544,128]{1,0:T(8,128)(2,1)S(1)}, u32[]{:S(2)}, u32[]{:S(2)}) collective-permute-start(bf16[544,128]{1,0:T(8,128)(2,1)S(1)} %get-tuple-element.8), channel_id=1, source_target_pairs={{1,2},{3,4},{5,6},{7,8},{9,10},{11,12},{13,14},{2,1},{4,3},{6,5},{... | collective-permute-start | bytes 417800 | tf_op jit(solution)/shard_map/ppermute | solution.py:556
  6.4 5.1 %collective-permute-start.1 = (bf16[544,128]{1,0:T(8,128)(2,1)S(1)}, bf16[544,128]{1,0:T(8,128)(2,1)S(1)}, u32[]{:S(2)}, u32[]{:S(2)}) collective-permute-start(bf16[544,128]{1,0:T(8,128)(2,1)S(1)} %get-tuple-element.9), channel_id=1, source_target_pairs={{0,1},{2,3},{4,5},{6,7},{8,9},{10,11},{12,13},{14,15},{1,0},{3,2},... | collective-permute-start | bytes 417800 | tf_op jit(solution)/shard_map/ppermute | solution.py:557
